TPU v7x, 128 devices: a whole 4x4x4 slice. The times are simulated.
128 devices in a mesh: gx: 8 (over z, y_hi), gy: 4 (over x), gz: 4 (over y_lo, core).
Axes of the slice: x: 4, y: 4 (y_hi: 2, y_lo: 2; y = y_hi * 2 + y_lo), z: 4, core: 2. Of those that a mesh axis runs over, the one named last changes fastest.
Arguments:
- checkpoint: float32 [256, 256, 1024], P('gx', 'gy', 'gz'), may hold values from -6 to 6
- diffusivity: float32 [256, 256, 1024], P('gx', 'gy', 'gz'), may hold values from 0.1 to 1
- material_scale: float32 [4], replicated, may hold values from 0.5 to 1
- labels: int32 [256, 256, 1024], P('gx', 'gy', 'gz'), may hold values from 0 to 3
- measured: float32 [256, 256, 1024], P('gx', 'gy', 'gz'), may hold values from -6 to 6
- observed: int32 [256, 256, 1024], P('gx', 'gy', 'gz'), may hold values 0 or 1
- adjoint_in: float32 [256, 256, 1024], P('gx', 'gy', 'gz'), may hold values from -4 to 4
Outputs:
- gradient: float32 [256, 256, 1024], P('gx', 'gy', 'gz')
- adjoint_start: float32 [256, 256, 1024], P('gx', 'gy', 'gz')
All inputs are finite; a program needn't handle non-finite values. No bound on the sum of `observed` on one device may be relied on, other than what follows from the above.
Results may differ from a plain program's by a relative error of at most 0.00002.
Values sent between devices are 32-bit elements; how exact they have to be, the bound alone decides.
A program may use at most 192 MiB of HBM per device.

v0:
```python
import jax
import jax.numpy as jnp
from jax import lax
from jax.sharding import PartitionSpec as P

ITERS = 4
MATERIALS = 4


RATE = 0.15


def with_halo(block, sides, width):
    for axis, dim in sides:
        count = lax.axis_size(axis)
        forward = [(i, i + 1) for i in range(count - 1)]
        backward = [(target, source) for source, target in forward]
        low = lax.ppermute(
            lax.slice_in_dim(block, block.shape[dim] - width, None, axis=dim), axis, forward
        )
        high = lax.ppermute(lax.slice_in_dim(block, 0, width, axis=dim), axis, backward)
        block = jnp.concatenate([low, block, high], axis=dim)
    return block


def neighbour(x, dim, off):
    parts = [slice(1, -1), slice(1, -1), slice(1, -1)]
    parts[dim] = slice(off, x.shape[dim] - 2 + off)
    return x[tuple(parts)]


def advance(field_pad, kappa_pad):
    centre = neighbour(field_pad, 0, 1)
    kcentre = neighbour(kappa_pad, 0, 1)
    total = jnp.zeros_like(centre)
    for dim in range(3):
        for off in (0, 2):
            total = total + 0.5 * (kcentre + neighbour(kappa_pad, dim, off)) * (
                neighbour(field_pad, dim, off) - centre
            )
    return centre + RATE * total


def grad_term(lam_pad, temp_pad):
    lcentre = neighbour(lam_pad, 0, 1)
    tcentre = neighbour(temp_pad, 0, 1)
    total = jnp.zeros_like(lcentre)
    for dim in range(3):
        for off in (0, 2):
            total = total + (neighbour(lam_pad, dim, off) - lcentre) * (
                neighbour(temp_pad, dim, off) - tcentre
            )
    return -0.5 * RATE * total


def adjoint_pad(lam):
    return with_halo(lam, (("gx", 0), ("gy", 1), ("gz", 2)), 1)


def shards(checkpoint, diffusivity, material_scale, labels, measured, observed, adjoint_in):
    factor = jnp.zeros_like(diffusivity)
    for label_value in range(MATERIALS):
        factor = factor + jnp.where(labels == label_value, material_scale[label_value], 0.0)
    kappa = diffusivity * factor
    history = []
    kappa_pad = with_halo(kappa, (("gx", 0), ("gy", 1), ("gz", 2)), 1)
    temp = checkpoint
    for step in range(ITERS):
        temp_pad = with_halo(temp, (("gx", 0), ("gy", 1), ("gz", 2)), 1)
        history.append(temp_pad)
        temp = advance(temp_pad, kappa_pad)
    lam = adjoint_in + observed.astype(jnp.float32) * (temp - measured)
    acc = jnp.zeros_like(checkpoint)
    for step in range(ITERS - 1, -1, -1):
        lam_pad = adjoint_pad(lam)
        acc = acc + grad_term(lam_pad, history[step])
        lam = advance(lam_pad, kappa_pad)
    return (acc * factor, lam)


def solution(mesh):
    placed = (
        P("gx", "gy", "gz"),
        P("gx", "gy", "gz"),
        P(),
        P("gx", "gy", "gz"),
        P("gx", "gy", "gz"),
        P("gx", "gy", "gz"),
        P("gx", "gy", "gz"),
    )
    return jax.shard_map(
        shards,
        mesh=mesh,
        in_specs=placed,
        out_specs=(P("gx", "gy", "gz"), P("gx", "gy", "gz")),
        check_vma=False,
    )
```

profile of v0, /device:TPU:113, one launch (start us, length us, event | category | flops | bytes accessed | tf_op | source)
XLA Modules:
  0.0 534.7 jit_solution(9335889581439064277)
XLA Ops:
  6.2 5.6 %fusion.60 = f32[32,64,256]{2,1,0:T(8,128)S(1)} fusion(f32[32,64,256]{2,1,0:T(8,128)} %param.8, f32[]{:T(128)} %bitcast.3, s32[32,64,256]{2,1,0:T(8,128)} %param.10, f32[]{:T(128)} %bitcast.2, f32[]{:T(128)} %bitcast.1, f32[]{:T(128)} %bitcast), kind=kLoop, calls=%fused_computation.233 | loop fusion | flops 6291456 | bytes 6291472 | tf_op jit(solution)/shard_map/mul | solution.py:64
  11.9 5.5 %collective-permute-start.2 = (f32[1,64,256]{2,1,0:T(8,128)S(1)}, f32[1,64,256]{2,1,0:T(8,128)S(1)}, u32[]{:S(2)}, u32[]{:S(2)}) collective-permute-start(f32[1,64,256]{2,1,0:T(8,128)S(1)} %get-tuple-element.57), channel_id=1, source_target_pairs={{16,0},{32,16},{48,32},{64,48},{80,64},{96,80},{112,96},{17,1},{33... | collective-permute-start | bytes 196616 | tf_op jit(solution)/shard_map/ppermute | solution.py:21
  19.4 3.1 collective-permute-start.5
  25.7 3.7 collective-permute-start.4
  33.0 2.4 copy.139
  36.5 5.8 %collective-permute-start.9 = (f32[34,66,1]{1,0,2:T(8,128)}, f32[34,66,1]{1,0,2:T(8,128)}, u32[]{:S(2)}, u32[]{:S(2)}) collective-permute-start(f32[34,66,1]{1,0,2:T(8,128)} %copy.135), channel_id=1, source_target_pairs={{0,1},{1,2},{2,3},{4,5},{5,6},{6,7},{8,9},{9,10},{10,11},{12,13},{... | collective-permute-start | bytes 26936 | tf_op jit(solution)/shard_map/ppermute | solution.py:18
  47.6 2.4 copy.137
  53.1 3.6 collective-permute-start.8
  64.9 15.7 %multiply_add_fusion.7 = (f32[32,64,256]{2,1,0:T(8,128)S(1)}, f32[32,64,256]{2,1,0:T(8,128)}, f32[32,64,256]{2,1,0:T(8,128)}) fusion(f32[32,64,256]{2,1,0:T(8,128)} %param.7, f32[1,64,256]{2,1,0:T(8,128)} %copy-done.25, f32[1,64,256]{2,1,0:T(8,128)} %copy-done.24, f32[34,64,256]{2,1,0:T(8,128)} %copy-done.7, f32[34,1,256]{2,1,0:T(1,128)} %copy-done.26, ...), kind=kLoop, calls=%fused_computation.231 | loop fusion | flops 30932992 | bytes 13151296 | tf_op jit(solution)/shard_map/add | solution.py:41
  80.7 5.2 collective-permute-start.13
  87.6 6.7 %collective-permute-done.12 = f32[1,64,256]{2,1,0:T(8,128)S(1)} collective-permute-done((f32[1,64,256]{2,1,0:T(8,128)S(1)}, f32[1,64,256]{2,1,0:T(8,128)S(1)}, u32[]{:S(2)}, u32[]{:S(2)}) %collective-permute-start.12) | collective-permute-done | bytes 65568 | tf_op jit(solution)/shard_map/ppermute | solution.py:18
  94.4 4.3 collective-permute-start.14
  100.0 3.4 collective-permute-done.15
  105.6 2.4 copy.149
  108.0 3.7 collective-permute-start.17
  112.9 3.3 collective-permute-start.16
  119.7 14.6 %multiply_add_fusion.6 = f32[32,64,256]{2,1,0:T(8,128)S(1)} fusion(f32[32,64,256]{2,1,0:T(8,128)} %copy-done, f32[32,64,256]{2,1,0:T(8,128)} %get-tuple-element.6, f32[32,64,256]{2,1,0:T(8,128)} %get-tuple-element.5, f32[1,64,256]{2,1,0:T(8,128)} %copy-done.11, f32[1,64,256]{2,1,0:T(8,128)} %copy-done.10, f32[34,1,256]{2,1,0:T(1,128)} %copy-done.28, ...), kind=kLoop, calls=%fused_computation.230 | loop fusion | flops 27787264 | bytes 10905120 | tf_op jit(solution)/shard_map/add | solution.py:41
  134.3 5.4 %collective-permute-start.19 = (f32[1,64,256]{2,1,0:T(8,128)S(1)}, f32[1,64,256]{2,1,0:T(8,128)S(1)}, u32[]{:S(2)}, u32[]{:S(2)}) collective-permute-start(f32[1,64,256]{2,1,0:T(8,128)S(1)} %get-tuple-element.53), channel_id=1, source_target_pairs={{16,0},{32,16},{48,32},{64,48},{80,64},{96,80},{112,96},{17,1},{33... | collective-permute-start | bytes 196616 | tf_op jit(solution)/shard_map/ppermute | solution.py:21
  141.1 5.2 collective-permute-done.18
  146.4 2.5 collective-permute-start.20
  150.3 3.4 collective-permute-done.21
  158.7 5.3 collective-permute-start.23
  164.0 2.4 copy.157
  166.4 4.0 collective-permute-start.22
  175.0 15.3 %multiply_add_fusion.5 = f32[32,64,256]{2,1,0:T(8,128)S(1)} fusion(f32[32,64,256]{2,1,0:T(8,128)} %copy-done.1, f32[32,64,256]{2,1,0:T(8,128)} %get-tuple-element.6, f32[32,64,256]{2,1,0:T(8,128)} %get-tuple-element.5, f32[1,64,256]{2,1,0:T(8,128)} %copy-done.13, f32[1,64,256]{2,1,0:T(8,128)} %copy-done.12, f32[34,1,256]{2,1,0:T(1,128)} %copy-done.30, ...), kind=kLoop, calls=%fused_computation.229 | loop fusion | flops 27787264 | bytes 10905120 | tf_op jit(solution)/shard_map/add | solution.py:41
  194.1 5.3 collective-permute-done.24
  199.5 3.4 collective-permute-start.26
  204.3 3.4 collective-permute-done.27
  210.3 2.4 copy.169
  212.7 4.1 collective-permute-start.29
  216.8 2.4 copy.167
  219.2 3.9 collective-permute-start.28
  227.8 18.4 %multiply_add_fusion.4 = f32[32,64,256]{2,1,0:T(8,128)S(1)} fusion(f32[32,64,256]{2,1,0:T(8,128)} %param.13, f32[32,64,256]{2,1,0:T(8,128)} %param.11, f32[32,64,256]{2,1,0:T(8,128)} %copy-done.2, f32[32,64,256]{2,1,0:T(8,128)} %get-tuple-element.6, f32[32,64,256]{2,1,0:T(8,128)} %get-tuple-element.5, s32[32,64,256]{2,1,0:T(8,128)} %param.12, ...), kind=kLoop, calls=%fused_computation.228 | loop fusion | flops 29884416 | bytes 17196576 | tf_op jit(solution)/shard_map/add | solution.py:72
  246.2 4.1 collective-permute-start.31
  251.9 5.3 collective-permute-done.30
  260.3 3.4 collective-permute-done.33
  266.3 2.4 copy.179
  268.7 4.3 collective-permute-start.35
  273.0 2.4 copy.177
  275.4 3.6 collective-permute-start.34
  283.6 15.0 %multiply_add_fusion.3 = f32[32,64,256]{2,1,0:T(8,128)S(1)} fusion(f32[32,64,256]{2,1,0:T(8,128)} %copy-done.3, f32[32,64,256]{2,1,0:T(8,128)} %get-tuple-element.6, f32[32,64,256]{2,1,0:T(8,128)} %get-tuple-element.5, f32[1,64,256]{2,1,0:T(8,128)} %copy-done.15, f32[1,64,256]{2,1,0:T(8,128)} %copy-done.14, f32[34,1,256]{2,1,0:T(1,128)} %copy-done.32, ...), kind=kLoop, calls=%fused_computation.227 | loop fusion | flops 27787264 | bytes 10905120 | tf_op jit(solution)/shard_map/add | solution.py:41
  301.9 5.2 collective-permute-done.36
  310.2 3.4 collective-permute-done.39
  316.2 2.4 copy.189
  318.6 5.3 collective-permute-start.41
  323.9 2.4 copy.187
  326.4 3.6 collective-permute-start.40
  334.5 14.4 %multiply_add_fusion.2 = f32[32,64,256]{2,1,0:T(8,128)S(1)} fusion(f32[32,64,256]{2,1,0:T(8,128)} %copy-done.4, f32[32,64,256]{2,1,0:T(8,128)} %get-tuple-element.6, f32[32,64,256]{2,1,0:T(8,128)} %get-tuple-element.5, f32[1,64,256]{2,1,0:T(8,128)} %copy-done.17, f32[1,64,256]{2,1,0:T(8,128)} %copy-done.16, f32[34,1,256]{2,1,0:T(1,128)} %copy-done.34, ...), kind=kLoop, calls=%fused_computation.226 | loop fusion | flops 27787264 | bytes 10905120 | tf_op jit(solution)/shard_map/add | solution.py:41
  349.0 4.1 collective-permute-start.43
  354.4 5.2 collective-permute-done.42
  362.7 3.4 collective-permute-done.45
  368.7 2.4 copy.199
  371.1 5.2 collective-permute-start.47
  376.2 2.4 copy.197
  378.7 3.2 collective-permute-start.46
  386.5 15.1 %multiply_add_fusion.1 = f32[32,64,256]{2,1,0:T(8,128)S(1)} fusion(f32[32,64,256]{2,1,0:T(8,128)} %copy-done.5, f32[32,64,256]{2,1,0:T(8,128)} %get-tuple-element.6, f32[32,64,256]{2,1,0:T(8,128)} %get-tuple-element.5, f32[1,64,256]{2,1,0:T(8,128)} %copy-done.19, f32[1,64,256]{2,1,0:T(8,128)} %copy-done.18, f32[34,1,256]{2,1,0:T(1,128)} %copy-done.36, ...), kind=kLoop, calls=%fused_computation.225 | loop fusion | flops 27787264 | bytes 10905120 | tf_op jit(solution)/shard_map/add | solution.py:41
  404.9 5.2 collective-permute-done.48
  413.2 3.4 collective-permute-done.51
  419.2 2.4 copy.209
  421.6 5.3 collective-permute-start.53
  426.9 2.4 copy.207
  429.3 3.3 collective-permute-start.52
  437.2 79.0 %multiply_multiply_fusion = f32[32,64,256]{2,1,0:T(8,128)} fusion(f32[32,64,256]{2,1,0:T(8,128)} %param.7, f32[1,64,256]{2,1,0:T(8,128)} %copy-done.25, f32[1,64,256]{2,1,0:T(8,128)} %copy-done.24, f32[32,64,256]{2,1,0:T(8,128)} %copy-done, f32[1,64,256]{2,1,0:T(8,128)} %copy-done.11, f32[1,64,256]{2,1,0:T(8,128)} %copy-done.10, ...), kind=kLoop, calls=%fused_computation.223 | loop fusion | flops 127926272 | bytes 24949008 | tf_op jit(solution)/shard_map/mul | solution.py:78
  516.2 18.2 %multiply_add_fusion = f32[32,64,256]{2,1,0:T(8,128)} fusion(f32[32,64,256]{2,1,0:T(8,128)} %copy-done.6, f32[32,64,256]{2,1,0:T(8,128)} %get-tuple-element.6, f32[32,64,256]{2,1,0:T(8,128)} %get-tuple-element.5, f32[1,64,256]{2,1,0:T(8,128)} %copy-done.21, f32[1,64,256]{2,1,0:T(8,128)} %copy-done.20, f32[34,1,256]{2,1,0:T(1,128)} %copy-done.38, ...), kind=kLoop, calls=%fused_computation.224 | loop fusion | flops 27787264 | bytes 10905120 | tf_op jit(solution)/shard_map/add | solution.py:41
  (250 shorter events, 116.2 us)
Async XLA Ops:
  1.5 17.8 %collective-permute-start.3 = (f32[1,64,256]{2,1,0:T(8,128)S(1)}, f32[1,64,256]{2,1,0:T(8,128)S(1)}, u32[]{:S(2)}, u32[]{:S(2)}) collective-permute-start(f32[1,64,256]{2,1,0:T(8,128)S(1)} %get-tuple-element.59), channel_id=1, source_target_pairs={{16,0},{32,16},{48,32},{64,48},{80,64},{96,80},{112,96},{17,1},{33... | collective-permute-start | bytes 196616 | tf_op jit(solution)/shard_map/ppermute | solution.py:21
  3.5 15.2 %collective-permute-start.1 = (f32[1,64,256]{2,1,0:T(8,128)S(1)}, f32[1,64,256]{2,1,0:T(8,128)S(1)}, u32[]{:S(2)}, u32[]{:S(2)}) collective-permute-start(f32[1,64,256]{2,1,0:T(8,128)S(1)} %get-tuple-element.60), channel_id=1, source_target_pairs={{0,16},{16,32},{32,48},{48,64},{64,80},{80,96},{96,112},{1,17},{17... | collective-permute-start | bytes 196616 | tf_op jit(solution)/shard_map/ppermute | solution.py:18
  11.9 12.0 %collective-permute-start.2 = (f32[1,64,256]{2,1,0:T(8,128)S(1)}, f32[1,64,256]{2,1,0:T(8,128)S(1)}, u32[]{:S(2)}, u32[]{:S(2)}) collective-permute-start(f32[1,64,256]{2,1,0:T(8,128)S(1)} %get-tuple-element.57), channel_id=1, source_target_pairs={{16,0},{32,16},{48,32},{64,48},{80,64},{96,80},{112,96},{17,1},{33... | collective-permute-start | bytes 196616 | tf_op jit(solution)/shard_map/ppermute | solution.py:21
  17.4 7.7 %collective-permute-start = (f32[1,64,256]{2,1,0:T(8,128)S(1)}, f32[1,64,256]{2,1,0:T(8,128)S(1)}, u32[]{:S(2)}, u32[]{:S(2)}) collective-permute-start(f32[1,64,256]{2,1,0:T(8,128)S(1)} %get-tuple-element.58), channel_id=1, source_target_pairs={{0,16},{16,32},{32,48},{48,64},{64,80},{80,96},{96,112},{1,17},{17... | collective-permute-start | bytes 196616 | tf_op jit(solution)/shard_map/ppermute | solution.py:18
  19.4 11.3 %collective-permute-start.5 = (f32[34,1,256]{2,0,1:T(8,128)S(1)}, f32[34,1,256]{2,0,1:T(8,128)S(1)}, u32[]{:S(2)}, u32[]{:S(2)}) collective-permute-start(f32[34,1,256]{2,0,1:T(8,128)S(1)} %copy.212), channel_id=1, source_target_pairs={{0,4},{4,8},{8,12},{1,5},{5,9},{9,13},{2,6},{6,10},{10,14},{3,7},{... | collective-permute-start | bytes 104456 | tf_op jit(solution)/shard_map/ppermute | solution.py:18
  22.6 8.2 %collective-permute-start.7 = (f32[34,1,256]{2,0,1:T(8,128)S(1)}, f32[34,1,256]{2,0,1:T(8,128)S(1)}, u32[]{:S(2)}, u32[]{:S(2)}) collective-permute-start(f32[34,1,256]{2,0,1:T(8,128)S(1)} %copy.214), channel_id=1, source_target_pairs={{4,0},{8,4},{12,8},{5,1},{9,5},{13,9},{6,2},{10,6},{14,10},{7,3},{... | collective-permute-start | bytes 104456 | tf_op jit(solution)/shard_map/ppermute | solution.py:21
  25.7 18.5 %collective-permute-start.4 = (f32[34,1,256]{2,0,1:T(8,128)S(1)}, f32[34,1,256]{2,0,1:T(8,128)}, u32[]{:S(2)}, u32[]{:S(2)}) collective-permute-start(f32[34,1,256]{2,0,1:T(8,128)S(1)} %copy.211), channel_id=1, source_target_pairs={{0,4},{4,8},{8,12},{1,5},{5,9},{9,13},{2,6},{6,10},{10,14},{3,7},{... | collective-permute-start | bytes 104456 | tf_op jit(solution)/shard_map/ppermute | solution.py:18
  29.4 15.6 %collective-permute-start.6 = (f32[34,1,256]{2,0,1:T(8,128)}, f32[34,1,256]{2,0,1:T(8,128)}, u32[]{:S(2)}, u32[]{:S(2)}) collective-permute-start(f32[34,1,256]{2,0,1:T(8,128)} %copy.213), channel_id=1, source_target_pairs={{4,0},{8,4},{12,8},{5,1},{9,5},{13,9},{6,2},{10,6},{14,10},{7,3},{... | collective-permute-start | bytes 104456 | tf_op jit(solution)/shard_map/ppermute | solution.py:21
  36.5 21.5 %collective-permute-start.9 = (f32[34,66,1]{1,0,2:T(8,128)}, f32[34,66,1]{1,0,2:T(8,128)}, u32[]{:S(2)}, u32[]{:S(2)}) collective-permute-start(f32[34,66,1]{1,0,2:T(8,128)} %copy.135), channel_id=1, source_target_pairs={{0,1},{1,2},{2,3},{4,5},{5,6},{6,7},{8,9},{9,10},{10,11},{12,13},{... | collective-permute-start | bytes 26936 | tf_op jit(solution)/shard_map/ppermute | solution.py:18
  42.3 14.5 %collective-permute-start.11 = (f32[34,66,1]{1,0,2:T(8,128)}, f32[34,66,1]{1,0,2:T(8,128)}, u32[]{:S(2)}, u32[]{:S(2)}) collective-permute-start(f32[34,66,1]{1,0,2:T(8,128)} %copy.139), channel_id=1, source_target_pairs={{1,0},{2,1},{3,2},{5,4},{6,5},{7,6},{9,8},{10,9},{11,10},{13,12},{... | collective-permute-start | bytes 26936 | tf_op jit(solution)/shard_map/ppermute | solution.py:21
  50.1 10.3 %collective-permute-start.10 = (f32[34,66,1]{1,0,2:T(8,128)}, f32[34,66,1]{1,0,2:T(8,128)}, u32[]{:S(2)}, u32[]{:S(2)}) collective-permute-start(f32[34,66,1]{1,0,2:T(8,128)} %copy.137), channel_id=1, source_target_pairs={{1,0},{2,1},{3,2},{5,4},{6,5},{7,6},{9,8},{10,9},{11,10},{13,12},{... | collective-permute-start | bytes 26936 | tf_op jit(solution)/shard_map/ppermute | solution.py:21
  53.1 9.6 %collective-permute-start.8 = (f32[34,66,1]{1,0,2:T(8,128)}, f32[34,66,1]{1,0,2:T(8,128)}, u32[]{:S(2)}, u32[]{:S(2)}) collective-permute-start(f32[34,66,1]{1,0,2:T(8,128)} %copy.131), channel_id=1, source_target_pairs={{0,1},{1,2},{2,3},{4,5},{5,6},{6,7},{8,9},{9,10},{10,11},{12,13},{... | collective-permute-start | bytes 26936 | tf_op jit(solution)/shard_map/ppermute | solution.py:18
  58.1 22.6 %copy-start.9 = (f32[34,66,1]{2,1,0:T(8,128)}, f32[34,66,1]{2,1,0:T(8,128)S(1)}, u32[]{:S(2)}) copy-start(f32[34,66,1]{2,1,0:T(8,128)S(1)} %copy.140) | copy-start | bytes 26932
  80.7 23.1 %copy-start = (f32[32,64,256]{2,1,0:T(8,128)}, f32[32,64,256]{2,1,0:T(8,128)S(1)}, u32[]{:S(2)}) copy-start(f32[32,64,256]{2,1,0:T(8,128)S(1)} %get-tuple-element.4) | copy-start | bytes 6291460
  80.7 6.9 %collective-permute-start.13 = (f32[1,64,256]{2,1,0:T(8,128)S(1)}, f32[1,64,256]{2,1,0:T(8,128)S(1)}, u32[]{:S(2)}, u32[]{:S(2)}) collective-permute-start(f32[1,64,256]{2,1,0:T(8,128)S(1)} %get-tuple-element.55), channel_id=1, source_target_pairs={{16,0},{32,16},{48,32},{64,48},{80,64},{96,80},{112,96},{17,1},{33... | collective-permute-start | bytes 196616 | tf_op jit(solution)/shard_map/ppermute | solution.py:21
  85.9 8.4 %collective-permute-start.12 = (f32[1,64,256]{2,1,0:T(8,128)S(1)}, f32[1,64,256]{2,1,0:T(8,128)S(1)}, u32[]{:S(2)}, u32[]{:S(2)}) collective-permute-start(f32[1,64,256]{2,1,0:T(8,128)S(1)} %get-tuple-element.56), channel_id=1, source_target_pairs={{0,16},{16,32},{32,48},{48,64},{64,80},{80,96},{96,112},{1,17},{17... | collective-permute-start | bytes 196616 | tf_op jit(solution)/shard_map/ppermute | solution.py:18
  87.6 16.2 %copy-start.10 = (f32[1,64,256]{2,1,0:T(8,128)}, f32[1,64,256]{2,1,0:T(8,128)S(1)}, u32[]{:S(2)}) copy-start(f32[1,64,256]{2,1,0:T(8,128)S(1)} %collective-permute-done.13) | copy-start | bytes 196612
  94.4 5.6 %collective-permute-start.14 = (f32[34,1,256]{2,0,1:T(8,128)S(1)}, f32[34,1,256]{2,0,1:T(8,128)S(1)}, u32[]{:S(2)}, u32[]{:S(2)}) collective-permute-start(f32[34,1,256]{2,0,1:T(8,128)S(1)} %copy.215), channel_id=1, source_target_pairs={{0,4},{4,8},{8,12},{1,5},{5,9},{9,13},{2,6},{6,10},{10,14},{3,7},{... | collective-permute-start | bytes 104456 | tf_op jit(solution)/shard_map/ppermute | solution.py:18
  98.7 4.7 collective-permute-start.15
  108.0 8.2 %collective-permute-start.17 = (f32[34,66,1]{1,0,2:T(8,128)}, f32[34,66,1]{1,0,2:T(8,128)}, u32[]{:S(2)}, u32[]{:S(2)}) collective-permute-start(f32[34,66,1]{1,0,2:T(8,128)} %copy.149), channel_id=1, source_target_pairs={{1,0},{2,1},{3,2},{5,4},{6,5},{7,6},{9,8},{10,9},{11,10},{13,12},{... | collective-permute-start | bytes 26936 | tf_op jit(solution)/shard_map/ppermute | solution.py:21
  112.9 4.6 collective-permute-start.16
  134.3 19.8 %copy-start.1 = (f32[32,64,256]{2,1,0:T(8,128)}, f32[32,64,256]{2,1,0:T(8,128)S(1)}, u32[]{:S(2)}) copy-start(f32[32,64,256]{2,1,0:T(8,128)S(1)} %multiply_add_fusion.6) | copy-start | bytes 6291460
  134.3 6.8 %collective-permute-start.19 = (f32[1,64,256]{2,1,0:T(8,128)S(1)}, f32[1,64,256]{2,1,0:T(8,128)S(1)}, u32[]{:S(2)}, u32[]{:S(2)}) collective-permute-start(f32[1,64,256]{2,1,0:T(8,128)S(1)} %get-tuple-element.53), channel_id=1, source_target_pairs={{16,0},{32,16},{48,32},{64,48},{80,64},{96,80},{112,96},{17,1},{33... | collective-permute-start | bytes 196616 | tf_op jit(solution)/shard_map/ppermute | solution.py:21
  139.8 6.5 %collective-permute-start.18 = (f32[1,64,256]{2,1,0:T(8,128)S(1)}, f32[1,64,256]{2,1,0:T(8,128)S(1)}, u32[]{:S(2)}, u32[]{:S(2)}) collective-permute-start(f32[1,64,256]{2,1,0:T(8,128)S(1)} %get-tuple-element.54), channel_id=1, source_target_pairs={{0,16},{16,32},{32,48},{48,64},{64,80},{80,96},{96,112},{1,17},{17... | collective-permute-start | bytes 196616 | tf_op jit(solution)/shard_map/ppermute | solution.py:18
  146.4 3.9 collective-permute-start.20
  148.9 4.8 collective-permute-start.21
  158.7 11.7 %collective-permute-start.23 = (f32[34,66,1]{1,0,2:T(8,128)}, f32[34,66,1]{1,0,2:T(8,128)}, u32[]{:S(2)}, u32[]{:S(2)}) collective-permute-start(f32[34,66,1]{1,0,2:T(8,128)} %copy.159), channel_id=1, source_target_pairs={{1,0},{2,1},{3,2},{5,4},{6,5},{7,6},{9,8},{10,9},{11,10},{13,12},{... | collective-permute-start | bytes 26936 | tf_op jit(solution)/shard_map/ppermute | solution.py:21
  166.4 6.4 %collective-permute-start.22 = (f32[34,66,1]{1,0,2:T(8,128)}, f32[34,66,1]{1,0,2:T(8,128)}, u32[]{:S(2)}, u32[]{:S(2)}) collective-permute-start(f32[34,66,1]{1,0,2:T(8,128)} %copy.157), channel_id=1, source_target_pairs={{0,1},{1,2},{2,3},{4,5},{5,6},{6,7},{8,9},{9,10},{10,11},{12,13},{... | collective-permute-start | bytes 26936 | tf_op jit(solution)/shard_map/ppermute | solution.py:18
  190.3 17.8 %copy-start.2 = (f32[32,64,256]{2,1,0:T(8,128)}, f32[32,64,256]{2,1,0:T(8,128)S(1)}, u32[]{:S(2)}) copy-start(f32[32,64,256]{2,1,0:T(8,128)S(1)} %multiply_add_fusion.5) | copy-start | bytes 6291460
  190.3 3.8 collective-permute-start.25
  192.3 7.2 %collective-permute-start.24 = (f32[1,64,256]{2,1,0:T(8,128)S(1)}, f32[1,64,256]{2,1,0:T(8,128)S(1)}, u32[]{:S(2)}, u32[]{:S(2)}) collective-permute-start(f32[1,64,256]{2,1,0:T(8,128)S(1)} %get-tuple-element.52), channel_id=1, source_target_pairs={{0,16},{16,32},{32,48},{48,64},{64,80},{80,96},{96,112},{1,17},{17... | collective-permute-start | bytes 196616 | tf_op jit(solution)/shard_map/ppermute | solution.py:18
  194.1 14.0 %copy-start.22 = (f32[1,64,256]{2,1,0:T(8,128)}, f32[1,64,256]{2,1,0:T(8,128)S(1)}, u32[]{:S(2)}) copy-start(f32[1,64,256]{2,1,0:T(8,128)S(1)} %collective-permute-done.25) | copy-start | bytes 196612
  199.5 4.7 collective-permute-start.26
  202.9 4.7 collective-permute-start.27
  212.7 10.4 %collective-permute-start.29 = (f32[34,66,1]{1,0,2:T(8,128)}, f32[34,66,1]{1,0,2:T(8,128)}, u32[]{:S(2)}, u32[]{:S(2)}) collective-permute-start(f32[34,66,1]{1,0,2:T(8,128)} %copy.169), channel_id=1, source_target_pairs={{1,0},{2,1},{3,2},{5,4},{6,5},{7,6},{9,8},{10,9},{11,10},{13,12},{... | collective-permute-start | bytes 26936 | tf_op jit(solution)/shard_map/ppermute | solution.py:21
  219.2 6.2 %collective-permute-start.28 = (f32[34,66,1]{1,0,2:T(8,128)}, f32[34,66,1]{1,0,2:T(8,128)}, u32[]{:S(2)}, u32[]{:S(2)}) collective-permute-start(f32[34,66,1]{1,0,2:T(8,128)} %copy.167), channel_id=1, source_target_pairs={{0,1},{1,2},{2,3},{4,5},{5,6},{6,7},{8,9},{9,10},{10,11},{12,13},{... | collective-permute-start | bytes 26936 | tf_op jit(solution)/shard_map/ppermute | solution.py:18
  246.2 17.9 %copy-start.3 = (f32[32,64,256]{2,1,0:T(8,128)}, f32[32,64,256]{2,1,0:T(8,128)S(1)}, u32[]{:S(2)}) copy-start(f32[32,64,256]{2,1,0:T(8,128)S(1)} %multiply_add_fusion.4) | copy-start | bytes 6291460
  246.2 5.7 %collective-permute-start.31 = (f32[1,64,256]{2,1,0:T(8,128)S(1)}, f32[1,64,256]{2,1,0:T(8,128)S(1)}, u32[]{:S(2)}, u32[]{:S(2)}) collective-permute-start(f32[1,64,256]{2,1,0:T(8,128)S(1)} %get-tuple-element.49), channel_id=1, source_target_pairs={{16,0},{32,16},{48,32},{64,48},{80,64},{96,80},{112,96},{17,1},{33... | collective-permute-start | bytes 196616 | tf_op jit(solution)/shard_map/ppermute | solution.py:21
  250.3 6.9 %collective-permute-start.30 = (f32[1,64,256]{2,1,0:T(8,128)S(1)}, f32[1,64,256]{2,1,0:T(8,128)S(1)}, u32[]{:S(2)}, u32[]{:S(2)}) collective-permute-start(f32[1,64,256]{2,1,0:T(8,128)S(1)} %get-tuple-element.50), channel_id=1, source_target_pairs={{0,16},{16,32},{32,48},{48,64},{64,80},{80,96},{96,112},{1,17},{17... | collective-permute-start | bytes 196616 | tf_op jit(solution)/shard_map/ppermute | solution.py:18
  257.3 3.0 collective-permute-start.32
  258.9 4.7 collective-permute-start.33
  268.7 10.4 %collective-permute-start.35 = (f32[34,66,1]{1,0,2:T(8,128)}, f32[34,66,1]{1,0,2:T(8,128)}, u32[]{:S(2)}, u32[]{:S(2)}) collective-permute-start(f32[34,66,1]{1,0,2:T(8,128)} %copy.179), channel_id=1, source_target_pairs={{1,0},{2,1},{3,2},{5,4},{6,5},{7,6},{9,8},{10,9},{11,10},{13,12},{... | collective-permute-start | bytes 26936 | tf_op jit(solution)/shard_map/ppermute | solution.py:21
  275.4 5.9 %collective-permute-start.34 = (f32[34,66,1]{1,0,2:T(8,128)}, f32[34,66,1]{1,0,2:T(8,128)}, u32[]{:S(2)}, u32[]{:S(2)}) collective-permute-start(f32[34,66,1]{1,0,2:T(8,128)} %copy.177), channel_id=1, source_target_pairs={{0,1},{1,2},{2,3},{4,5},{5,6},{6,7},{8,9},{9,10},{10,11},{12,13},{... | collective-permute-start | bytes 26936 | tf_op jit(solution)/shard_map/ppermute | solution.py:18
  298.6 15.3 %copy-start.4 = (f32[32,64,256]{2,1,0:T(8,128)}, f32[32,64,256]{2,1,0:T(8,128)S(1)}, u32[]{:S(2)}) copy-start(f32[32,64,256]{2,1,0:T(8,128)S(1)} %multiply_add_fusion.3) | copy-start | bytes 6291460
  298.7 3.3 collective-permute-start.37
  300.6 6.5 %collective-permute-start.36 = (f32[1,64,256]{2,1,0:T(8,128)S(1)}, f32[1,64,256]{2,1,0:T(8,128)S(1)}, u32[]{:S(2)}, u32[]{:S(2)}) collective-permute-start(f32[1,64,256]{2,1,0:T(8,128)S(1)} %get-tuple-element.48), channel_id=1, source_target_pairs={{0,16},{16,32},{32,48},{48,64},{64,80},{80,96},{96,112},{1,17},{17... | collective-permute-start | bytes 196616 | tf_op jit(solution)/shard_map/ppermute | solution.py:18
  307.2 3.0 collective-permute-start.38
  308.9 4.7 collective-permute-start.39
  318.6 11.4 %collective-permute-start.41 = (f32[34,66,1]{1,0,2:T(8,128)}, f32[34,66,1]{1,0,2:T(8,128)}, u32[]{:S(2)}, u32[]{:S(2)}) collective-permute-start(f32[34,66,1]{1,0,2:T(8,128)} %copy.189), channel_id=1, source_target_pairs={{1,0},{2,1},{3,2},{5,4},{6,5},{7,6},{9,8},{10,9},{11,10},{13,12},{... | collective-permute-start | bytes 26936 | tf_op jit(solution)/shard_map/ppermute | solution.py:21
  326.4 5.9 %collective-permute-start.40 = (f32[34,66,1]{1,0,2:T(8,128)}, f32[34,66,1]{1,0,2:T(8,128)}, u32[]{:S(2)}, u32[]{:S(2)}) collective-permute-start(f32[34,66,1]{1,0,2:T(8,128)} %copy.187), channel_id=1, source_target_pairs={{0,1},{1,2},{2,3},{4,5},{5,6},{6,7},{8,9},{9,10},{10,11},{12,13},{... | collective-permute-start | bytes 26936 | tf_op jit(solution)/shard_map/ppermute | solution.py:18
  349.0 17.5 %copy-start.5 = (f32[32,64,256]{2,1,0:T(8,128)}, f32[32,64,256]{2,1,0:T(8,128)S(1)}, u32[]{:S(2)}) copy-start(f32[32,64,256]{2,1,0:T(8,128)S(1)} %multiply_add_fusion.2) | copy-start | bytes 6291460
  349.0 5.4 %collective-permute-start.43 = (f32[1,64,256]{2,1,0:T(8,128)S(1)}, f32[1,64,256]{2,1,0:T(8,128)S(1)}, u32[]{:S(2)}, u32[]{:S(2)}) collective-permute-start(f32[1,64,256]{2,1,0:T(8,128)S(1)} %get-tuple-element.45), channel_id=1, source_target_pairs={{16,0},{32,16},{48,32},{64,48},{80,64},{96,80},{112,96},{17,1},{33... | collective-permute-start | bytes 196616 | tf_op jit(solution)/shard_map/ppermute | solution.py:21
  353.1 6.5 %collective-permute-start.42 = (f32[1,64,256]{2,1,0:T(8,128)S(1)}, f32[1,64,256]{2,1,0:T(8,128)S(1)}, u32[]{:S(2)}, u32[]{:S(2)}) collective-permute-start(f32[1,64,256]{2,1,0:T(8,128)S(1)} %get-tuple-element.46), channel_id=1, source_target_pairs={{0,16},{16,32},{32,48},{48,64},{64,80},{80,96},{96,112},{1,17},{17... | collective-permute-start | bytes 196616 | tf_op jit(solution)/shard_map/ppermute | solution.py:18
  359.7 3.0 collective-permute-start.44
  361.3 4.7 collective-permute-start.45
  371.1 10.8 %collective-permute-start.47 = (f32[34,66,1]{1,0,2:T(8,128)}, f32[34,66,1]{1,0,2:T(8,128)}, u32[]{:S(2)}, u32[]{:S(2)}) collective-permute-start(f32[34,66,1]{1,0,2:T(8,128)} %copy.199), channel_id=1, source_target_pairs={{1,0},{2,1},{3,2},{5,4},{6,5},{7,6},{9,8},{10,9},{11,10},{13,12},{... | collective-permute-start | bytes 26936 | tf_op jit(solution)/shard_map/ppermute | solution.py:21
  378.7 5.5 %collective-permute-start.46 = (f32[34,66,1]{1,0,2:T(8,128)}, f32[34,66,1]{1,0,2:T(8,128)}, u32[]{:S(2)}, u32[]{:S(2)}) collective-permute-start(f32[34,66,1]{1,0,2:T(8,128)} %copy.197), channel_id=1, source_target_pairs={{0,1},{1,2},{2,3},{4,5},{5,6},{6,7},{8,9},{9,10},{10,11},{12,13},{... | collective-permute-start | bytes 26936 | tf_op jit(solution)/shard_map/ppermute | solution.py:18
  401.6 15.3 %copy-start.6 = (f32[32,64,256]{2,1,0:T(8,128)}, f32[32,64,256]{2,1,0:T(8,128)S(1)}, u32[]{:S(2)}) copy-start(f32[32,64,256]{2,1,0:T(8,128)S(1)} %multiply_add_fusion.1) | copy-start | bytes 6291460
  401.7 3.3 collective-permute-start.49
  403.6 6.5 %collective-permute-start.48 = (f32[1,64,256]{2,1,0:T(8,128)S(1)}, f32[1,64,256]{2,1,0:T(8,128)S(1)}, u32[]{:S(2)}, u32[]{:S(2)}) collective-permute-start(f32[1,64,256]{2,1,0:T(8,128)S(1)} %get-tuple-element.44), channel_id=1, source_target_pairs={{0,16},{16,32},{32,48},{48,64},{64,80},{80,96},{96,112},{1,17},{17... | collective-permute-start | bytes 196616 | tf_op jit(solution)/shard_map/ppermute | solution.py:18
  410.2 3.0 collective-permute-start.50
  411.8 4.7 collective-permute-start.51
  421.6 11.1 %collective-permute-start.53 = (f32[34,66,1]{1,0,2:T(8,128)}, f32[34,66,1]{1,0,2:T(8,128)}, u32[]{:S(2)}, u32[]{:S(2)}) collective-permute-start(f32[34,66,1]{1,0,2:T(8,128)} %copy.209), channel_id=1, source_target_pairs={{1,0},{2,1},{3,2},{5,4},{6,5},{7,6},{9,8},{10,9},{11,10},{13,12},{... | collective-permute-start | bytes 26936 | tf_op jit(solution)/shard_map/ppermute | solution.py:21
  429.3 5.6 %collective-permute-start.52 = (f32[34,66,1]{1,0,2:T(8,128)}, f32[34,66,1]{1,0,2:T(8,128)}, u32[]{:S(2)}, u32[]{:S(2)}) collective-permute-start(f32[34,66,1]{1,0,2:T(8,128)} %copy.207), channel_id=1, source_target_pairs={{0,1},{1,2},{2,3},{4,5},{5,6},{6,7},{8,9},{9,10},{10,11},{12,13},{... | collective-permute-start | bytes 26936 | tf_op jit(solution)/shard_map/ppermute | solution.py:18
  (32 other events, 183.8 us)
where the time goes:
time: 545 us; the launch traced here: 535 us
  other arithmetic  215 us (39%)
  starting transfers between devices  150 us (28%)
  local copies, waits for them, and re-layouts  103 us (19%)
  waiting for transfers between devices  64.4 us (12%)
    add x7, other arithmetic, advance(): return centre + RATE * total  108 us
    ppermute x27, starting transfers between devices, with_halo(): lax.ppermute(lax.slice_in_dim(block, 0, width, axis=dim), axis, backward)  80.6 us
    mul x1, other arithmetic, shards(): return (acc * factor, lam)  79 us
    ppermute x27, starting transfers between devices, with_halo(): lax.ppermute(lax.slice_in_dim(block, block.shape[dim] - width, None, axis...  69.6 us
    ppermute x27, waiting for transfers between devices, with_halo(): lax.ppermute(lax.slice_in_dim(block, block.shape[dim] - width, None, axis...  39.4 us
    slice x28, local copies, waits for them, and re-layouts, with_halo(): lax.slice_in_dim(block, 0, width, axis=dim)  38.3 us
    ppermute x27, waiting for transfers between devices, with_halo(): lax.ppermute(lax.slice_in_dim(block, 0, width, axis=dim), axis, backward)  25 us
    ppermute x18, local copies, waits for them, and re-layouts, with_halo(): lax.ppermute(lax.slice_in_dim(block, block.shape[dim] - width, None, axis...  21.6 us
  transfers between devices with their start and end apart: 54, of which 18 were waited for; matrix products, arithmetic and copies ran while one was open for 11% of the time, Pallas kernels for 0%

commit v1 on v0

v1 whole, which is shorter than its diff:
```python
import functools

import jax
import jax.numpy as jnp
from jax import lax
from jax.experimental import pallas as pl
from jax.experimental.pallas import tpu as pltpu
from jax.sharding import PartitionSpec as P

ITERS = 4
MATERIALS = 4

RATE = 0.15
HALF_RATE = 0.5 * RATE
AXES = ("gx", "gy", "gz")
LANES = 128
VMEM_LIMIT = 56 * 1024 * 1024
MESH_ID = pl.DeviceIdType.MESH


def _vmem():
    return pl.BlockSpec(memory_space=pltpu.VMEM)


def _smem():
    return pl.BlockSpec(memory_space=pltpu.SMEM)


class Geo:
    def __init__(self, shape):
        self.X, self.Y, self.Z = shape
        self.row = lax.broadcasted_iota(jnp.int32, (self.Y, self.Z), 0)
        self.lane = lax.broadcasted_iota(jnp.int32, (self.Y, self.Z), 1)
        self.lane128 = lax.broadcasted_iota(jnp.int32, (self.Y, LANES), 1)

    def widen(self, v):
        return jnp.concatenate([v] * (self.Z // LANES), axis=1)


def _slab_nbrs(g, F, halo, x, pos):
    xh, yh, zh = halo
    c = F[x]
    xm = xh[0] if pos == "first" else F[x - 1]
    xp = xh[1] if pos == "last" else F[x + 1]
    ym = jnp.where(g.row == 0, yh[0, pl.ds(x, 1), :], pltpu.roll(c, 1, 0))
    yp = jnp.where(g.row == g.Y - 1, yh[1, pl.ds(x, 1), :], pltpu.roll(c, g.Y - 1, 0))
    zlo = pltpu.roll(zh[0], lax.rem(LANES - x, LANES), 1)
    zhi = pltpu.roll(zh[1], lax.rem(LANES - 1 - x + LANES, LANES), 1)
    zm = jnp.where(g.lane == 0, g.widen(zlo), pltpu.roll(c, 1, 1))
    zp = jnp.where(g.lane == g.Z - 1, g.widen(zhi), pltpu.roll(c, g.Z - 1, 1))
    return c, (xm, xp, ym, yp, zm, zp)


def _pack(g, faces, x, new, pos):
    xs, ys, zs = faces
    if pos == "first":
        xs[0] = new
    if pos == "last":
        xs[1] = new
    ys[0, pl.ds(x, 1), :] = new[0:1, :]
    ys[1, pl.ds(x, 1), :] = new[g.Y - 1 : g.Y, :]
    w0 = pltpu.roll(new[:, 0:LANES], x, 1)
    w1 = pltpu.roll(new[:, g.Z - LANES : g.Z], lax.rem(x + 1, LANES), 1)
    zs[0] = jnp.where(g.lane128 == x, w0, zs[0])
    zs[1] = jnp.where(g.lane128 == x, w1, zs[1])


def _zero_faces(faces):
    zs = faces[2]
    zs[...] = jnp.zeros(zs.shape, zs.dtype)


def _over_slabs(X, body):
    body(0, "first")
    if X > 2:

        def step(x, carry):
            body(x, "mid")
            return carry

        lax.fori_loop(1, X - 1, step, 0)
    body(X - 1, "last")


def _factor(scale, lab):
    f = jnp.where(lab == 2, scale[2], scale[3])
    f = jnp.where(lab == 1, scale[1], f)
    return jnp.where(lab == 0, scale[0], f)


def _stencil(c, nb, kc, knb):
    total = jnp.zeros_like(c)
    for v, k in zip(nb, knb):
        total = total + (kc + k) * (v - c)
    return c + HALF_RATE * total


def _prep_kernel(diff, labels, scale, ckpt, kap, xs, ys, zs):
    g = Geo(diff.shape)
    kf = (xs.at[0], ys.at[0], zs.at[0])
    uf = (xs.at[1], ys.at[1], zs.at[1])
    _zero_faces((xs, ys, zs))

    def body(x, pos):
        k = diff[x] * _factor(scale, labels[x])
        kap[x] = k
        _pack(g, kf, x, k, pos)
        _pack(g, uf, x, ckpt[x], pos)

    _over_slabs(g.X, body)


def _fwd_kernel(last, u, uxh, uyh, uzh, kap, kxh, kyh, kzh, *rest):
    if last:
        adj, obs, meas, out, xs, ys, zs = rest
    else:
        out, xs, ys, zs = rest
    g = Geo(u.shape)
    faces = (xs, ys, zs)
    _zero_faces(faces)

    def body(x, pos):
        c, nb = _slab_nbrs(g, u, (uxh, uyh, uzh), x, pos)
        kc, knb = _slab_nbrs(g, kap, (kxh, kyh, kzh), x, pos)
        new = _stencil(c, nb, kc, knb)
        if last:
            new = adj[x] + obs[x].astype(jnp.float32) * (new - meas[x])
        out[x] = new
        _pack(g, faces, x, new, pos)

    _over_slabs(g.X, body)


def _bwd_kernel(first, final, lam, lxh, lyh, lzh, u, uxh, uyh, uzh, kap, kxh, kyh, kzh, *rest):
    rest = list(rest)
    acc_in = None if first else rest.pop(0)
    if final:
        labels, scale, lam_out, acc_out = rest
        faces = None
    else:
        lam_out, acc_out, xs, ys, zs = rest
        faces = (xs, ys, zs)
        _zero_faces(faces)
    g = Geo(lam.shape)

    def body(x, pos):
        lc, lnb = _slab_nbrs(g, lam, (lxh, lyh, lzh), x, pos)
        uc, unb = _slab_nbrs(g, u, (uxh, uyh, uzh), x, pos)
        kc, knb = _slab_nbrs(g, kap, (kxh, kyh, kzh), x, pos)
        s = jnp.zeros_like(lc)
        t = jnp.zeros_like(lc)
        for lj, uj, kj in zip(lnb, unb, knb):
            d = lj - lc
            s = s + (kc + kj) * d
            t = t + d * (uj - uc)
        new = lc + HALF_RATE * s
        term = (-HALF_RATE) * t
        acc = term if first else acc_in[x] + term
        if final:
            acc = acc * _factor(scale, labels[x])
        acc_out[x] = acc
        lam_out[x] = new
        if faces is not None:
            _pack(g, faces, x, new, pos)

    _over_slabs(g.X, body)


def _comm_kernel(sizes, xs, ys, zs, xh, yh, zh, send_sem, recv_sem):
    nf = xs.shape[0]
    idx = [lax.axis_index(a) for a in AXES]

    def nbr(a, d):
        coords = list(idx)
        coords[a] = idx[a] + d
        return tuple(coords)

    def has(a, d):
        return jnp.logical_and(idx[a] + d >= 0, idx[a] + d < sizes[a])

    barrier = pltpu.get_barrier_semaphore()
    count = jnp.int32(0)
    for a in range(3):
        for d in (-1, 1):

            @pl.when(has(a, d))
            def _():
                pl.semaphore_signal(barrier, 1, device_id=nbr(a, d), device_id_type=MESH_ID)

            count = count + has(a, d).astype(jnp.int32)
    pl.semaphore_wait(barrier, count)

    bufs = ((xs, xh), (ys, yh), (zs, zh))
    for a, (_, dst) in enumerate(bufs):
        for s, d in ((0, -1), (1, 1)):

            @pl.when(jnp.logical_not(has(a, d)))
            def _():
                dst[:, s] = jnp.zeros(dst.shape[:1] + dst.shape[2:], dst.dtype)

    def copy(f, a, s):
        src, dst = bufs[a]
        k = 2 * a + s
        d = 1 if s == 0 else -1
        return pltpu.make_async_remote_copy(
            src_ref=src.at[f, 1 - s],
            dst_ref=dst.at[f, s],
            send_sem=send_sem.at[f, k],
            recv_sem=recv_sem.at[f, k],
            device_id=nbr(a, d),
            device_id_type=MESH_ID,
        )

    for f in range(nf):
        for a in range(3):
            for s in (0, 1):
                d = 1 if s == 0 else -1

                @pl.when(has(a, d))
                def _():
                    copy(f, a, s).start()

    for f in range(nf):
        for a in range(3):
            for s in (0, 1):
                d_send = 1 if s == 0 else -1
                d_recv = -1 if s == 0 else 1

                @pl.when(has(a, d_recv))
                def _():
                    copy(f, a, s).wait_recv()

                @pl.when(has(a, d_send))
                def _():
                    copy(f, a, s).wait_send()


def _face_shapes(shape, nf=None):
    X, Y, Z = shape
    lead = (2,) if nf is None else (nf, 2)
    return (
        jax.ShapeDtypeStruct(lead + (Y, Z), jnp.float32),
        jax.ShapeDtypeStruct(lead + (X, Z), jnp.float32),
        jax.ShapeDtypeStruct(lead + (Y, LANES), jnp.float32),
    )


def _params(**kw):
    return pltpu.CompilerParams(vmem_limit_bytes=VMEM_LIMIT, **kw)


def _call(kernel, n_in, out_shape, smem_at=(), **kw):
    in_specs = [_smem() if i in smem_at else _vmem() for i in range(n_in)]
    return pl.pallas_call(
        kernel,
        out_shape=out_shape,
        in_specs=in_specs,
        out_specs=tuple(_vmem() for _ in out_shape),
        compiler_params=_params(**kw),
    )


def _exchange(sizes, faces):
    xs, ys, zs = faces
    nf = xs.shape[0]
    out_shape = (
        jax.ShapeDtypeStruct(xs.shape, xs.dtype),
        jax.ShapeDtypeStruct(ys.shape, ys.dtype),
        jax.ShapeDtypeStruct(zs.shape, zs.dtype),
    )
    return pl.pallas_call(
        functools.partial(_comm_kernel, sizes),
        out_shape=out_shape,
        in_specs=[_vmem()] * 3,
        out_specs=tuple(_vmem() for _ in out_shape),
        scratch_shapes=[pltpu.SemaphoreType.DMA((nf, 6)), pltpu.SemaphoreType.DMA((nf, 6))],
        compiler_params=_params(collective_id=nf - 1, has_side_effects=True),
    )(xs, ys, zs)


def _pick(h, f):
    return tuple(a[f] for a in h)


def _shards(sizes, checkpoint, diffusivity, material_scale, labels, measured, observed, adjoint_in):
    shape = checkpoint.shape
    field = jax.ShapeDtypeStruct(shape, jnp.float32)

    kap, xs, ys, zs = _call(_prep_kernel, 4, (field,) + _face_shapes(shape, 2), smem_at=(2,))(
        diffusivity, labels, material_scale, checkpoint
    )
    h = _exchange(sizes, (xs, ys, zs))
    kh = _pick(h, 0)
    uh = [_pick(h, 1)]
    us = [checkpoint]

    for n in range(ITERS):
        last = n == ITERS - 1
        extra = (adjoint_in, observed, measured) if last else ()
        new, xs, ys, zs = _call(
            functools.partial(_fwd_kernel, last), 8 + len(extra), (field,) + _face_shapes(shape)
        )(us[n], *uh[n], kap, *kh, *extra)
        h = _exchange(sizes, (xs[None], ys[None], zs[None]))
        if last:
            lam, lh = new, _pick(h, 0)
        else:
            us.append(new)
            uh.append(_pick(h, 0))

    acc = None
    for n in range(ITERS - 1, -1, -1):
        first = n == ITERS - 1
        final = n == 0
        ins = [lam, *lh, us[n], *uh[n], kap, *kh]
        if not first:
            ins.append(acc)
        if final:
            ins += [labels, material_scale]
            outs = (field, field)
            smem_at = (len(ins) - 1,)
        else:
            outs = (field, field) + _face_shapes(shape)
            smem_at = ()
        res = _call(functools.partial(_bwd_kernel, first, final), len(ins), outs, smem_at=smem_at)(*ins)
        if final:
            lam, acc = res
        else:
            lam, acc, xs, ys, zs = res
            h = _exchange(sizes, (xs[None], ys[None], zs[None]))
            lh = _pick(h, 0)
    return acc, lam


def solution(mesh):
    sizes = tuple(mesh.shape[a] for a in AXES)
    block = P("gx", "gy", "gz")
    placed = (block, block, P(), block, block, block, block)
    return jax.shard_map(
        functools.partial(_shards, sizes),
        mesh=mesh,
        in_specs=placed,
        out_specs=(block, block),
        check_vma=False,
    )
```

time: 545 us -> 203 us (0.37)
  the two profiles are of different devices: /device:TPU:113 before, /device:TPU:0 now
where the time goes in v1:
time: 203 us; the launch traced here: 202 us
  Pallas kernels  197 us (97%)
  local copies, waits for them, and re-layouts  4.73 us (2%)
    pallas_call x8, Pallas kernels, _exchange(): pl.pallas_call(functools.partial(_comm_kernel, sizes), out_shape=out_shap...  79.2 us
    pallas_call x4, Pallas kernels, _shards(): _call(functools.partial(_bwd_kernel, first, final), len(ins), outs, smem_...  60.6 us
    pallas_call x4, Pallas kernels, _shards(): _call(functools.partial(_fwd_kernel, last), 8 + len(extra), (field,) + _f...  49.3 us
    pallas_call x1, Pallas kernels, _shards(): _call(_prep_kernel, 4, (field,) + _face_shapes(shape, 2), smem_at=(2,))  7.61 us
    squeeze x3, local copies, waits for them, and re-layouts, _pick(): return tuple((a[f] for a in h))  4.73 us

profile of v1, /device:TPU:0, one launch (start us, length us, event | category | flops | bytes accessed | tf_op | source)
XLA Modules:
  0.0 202.1 jit_solution(4816736354933379510)
XLA Ops:
  0.6 7.6 %shard_map.86 = (f32[32,64,256]{2,1,0:T(8,128)}, f32[2,2,64,256]{3,2,1,0:T(8,128)}, f32[2,2,32,256]{3,2,1,0:T(8,128)}, f32[2,2,64,128]{3,2,1,0:T(8,128)}) custom-call(f32[32,64,256]{2,1,0:T(8,128)} %diff.1, s32[32,64,256]{2,1,0:T(8,128)} %rest_1_.3, f32[4]{0:T(128)} %rest_2_.3, f32[32,64,256]{2,1,0:T(8,128)} %u.3), custom_call_target="tpu_custom_call" | custom-call | tf_op jit(solution)/shard_map/pallas_call | solution.py:289
  8.2 13.9 %shard_map.87 = (f32[2,2,64,256]{3,2,1,0:T(8,128)}, f32[2,2,32,256]{3,2,1,0:T(8,128)}, f32[2,2,64,128]{3,2,1,0:T(8,128)}) custom-call(f32[2,2,64,256]{3,2,1,0:T(8,128)} %get-tuple-element.63.xs, f32[2,2,32,256]{3,2,1,0:T(8,128)} %get-tuple-element.64.ys, f32[2,2,64,128]{3,2,1,0:T(8,128)} %get-tuple-element.65.zs), custom_call_target="tpu_custom_call" | custom-call | tf_op jit(solution)/shard_map/pallas_call | solution.py:271
  22.2 1.7 slice_bitcast_fusion
  23.9 1.5 slice_bitcast_fusion.3
  25.4 1.5 slice_bitcast_fusion.2
  26.9 11.7 %shard_map.88 = (f32[32,64,256]{2,1,0:T(8,128)}, f32[2,64,256]{2,1,0:T(8,128)}, f32[2,32,256]{2,1,0:T(8,128)}, f32[2,64,128]{2,1,0:T(8,128)}) custom-call(f32[32,64,256]{2,1,0:T(8,128)} %u.3, f32[2,64,256]{2,1,0:T(8,128)} %get-tuple-element.125.uxh, f32[2,32,256]{2,1,0:T(8,128)} %get-tuple-element.129.uyh, f32[2,64,128]{2,1,0:T(8,128)} %get-tuple-element.127.uzh, ...), custom_call_target="tpu_custom_call" | custom-call | tf_op jit(solution)/shard_map/pallas_call | solution.py:300
  38.6 9.9 %shard_map.89 = (f32[1,2,64,256]{3,2,1,0:T(8,128)}, f32[1,2,32,256]{3,2,1,0:T(8,128)}, f32[1,2,64,128]{3,2,1,0:T(8,128)}) custom-call(f32[1,2,64,256]{3,2,1,0:T(8,128)} %bitcast.79, f32[1,2,32,256]{3,2,1,0:T(8,128)} %bitcast.97, f32[1,2,64,128]{3,2,1,0:T(8,128)} %bitcast.98), custom_call_target="tpu_custom_call" | custom-call | tf_op jit(solution)/shard_map/pallas_call | solution.py:271
  48.5 11.7 %shard_map.90 = (f32[32,64,256]{2,1,0:T(8,128)}, f32[2,64,256]{2,1,0:T(8,128)}, f32[2,32,256]{2,1,0:T(8,128)}, f32[2,64,128]{2,1,0:T(8,128)}) custom-call(f32[32,64,256]{2,1,0:T(8,128)} %get-tuple-element.70.u, f32[2,64,256]{2,1,0:T(8,128)} %bitcast.56, f32[2,32,256]{2,1,0:T(8,128)} %bitcast.60, f32[2,64,128]{2,1,0:T(8,128)} %bitcast.62, ...), custom_call_target="tpu_custom_call" | custom-call | tf_op jit(solution)/shard_map/pallas_call | solution.py:300
  60.2 9.6 %shard_map.91 = (f32[1,2,64,256]{3,2,1,0:T(8,128)}, f32[1,2,32,256]{3,2,1,0:T(8,128)}, f32[1,2,64,128]{3,2,1,0:T(8,128)}) custom-call(f32[1,2,64,256]{3,2,1,0:T(8,128)} %bitcast.80, f32[1,2,32,256]{3,2,1,0:T(8,128)} %bitcast.99, f32[1,2,64,128]{3,2,1,0:T(8,128)} %bitcast.100), custom_call_target="tpu_custom_call" | custom-call | tf_op jit(solution)/shard_map/pallas_call | solution.py:271
  69.8 11.8 %shard_map.92 = (f32[32,64,256]{2,1,0:T(8,128)}, f32[2,64,256]{2,1,0:T(8,128)}, f32[2,32,256]{2,1,0:T(8,128)}, f32[2,64,128]{2,1,0:T(8,128)}) custom-call(f32[32,64,256]{2,1,0:T(8,128)} %get-tuple-element.77.u, f32[2,64,256]{2,1,0:T(8,128)} %bitcast.58, f32[2,32,256]{2,1,0:T(8,128)} %bitcast.64, f32[2,64,128]{2,1,0:T(8,128)} %bitcast.66, ...), custom_call_target="tpu_custom_call" | custom-call | tf_op jit(solution)/shard_map/pallas_call | solution.py:300
  81.7 9.3 %shard_map.93 = (f32[1,2,64,256]{3,2,1,0:T(8,128)}, f32[1,2,32,256]{3,2,1,0:T(8,128)}, f32[1,2,64,128]{3,2,1,0:T(8,128)}) custom-call(f32[1,2,64,256]{3,2,1,0:T(8,128)} %bitcast.81, f32[1,2,32,256]{3,2,1,0:T(8,128)} %bitcast.101, f32[1,2,64,128]{3,2,1,0:T(8,128)} %bitcast.102), custom_call_target="tpu_custom_call" | custom-call | tf_op jit(solution)/shard_map/pallas_call | solution.py:271
  91.0 14.0 %shard_map.94 = (f32[32,64,256]{2,1,0:T(8,128)}, f32[2,64,256]{2,1,0:T(8,128)}, f32[2,32,256]{2,1,0:T(8,128)}, f32[2,64,128]{2,1,0:T(8,128)}) custom-call(f32[32,64,256]{2,1,0:T(8,128)} %get-tuple-element.84.u, f32[2,64,256]{2,1,0:T(8,128)} %bitcast.54, f32[2,32,256]{2,1,0:T(8,128)} %bitcast.68, f32[2,64,128]{2,1,0:T(8,128)} %bitcast.70, ...), custom_call_target="tpu_custom_call" | custom-call | tf_op jit(solution)/shard_map/pallas_call | solution.py:300
  104.9 9.2 %shard_map.95 = (f32[1,2,64,256]{3,2,1,0:T(8,128)}, f32[1,2,32,256]{3,2,1,0:T(8,128)}, f32[1,2,64,128]{3,2,1,0:T(8,128)}) custom-call(f32[1,2,64,256]{3,2,1,0:T(8,128)} %bitcast.82, f32[1,2,32,256]{3,2,1,0:T(8,128)} %bitcast.103, f32[1,2,64,128]{3,2,1,0:T(8,128)} %bitcast.104), custom_call_target="tpu_custom_call" | custom-call | tf_op jit(solution)/shard_map/pallas_call | solution.py:271
  114.1 15.0 %shard_map.96 = (f32[32,64,256]{2,1,0:T(8,128)}, f32[32,64,256]{2,1,0:T(8,128)}, f32[2,64,256]{2,1,0:T(8,128)}, f32[2,32,256]{2,1,0:T(8,128)}, f32[2,64,128]{2,1,0:T(8,128)}) custom-call(f32[32,64,256]{2,1,0:T(8,128)} %get-tuple-element.91.lam, f32[2,64,256]{2,1,0:T(8,128)} %bitcast.75, f32[2,32,256]{2,1,0:T(8,128)} %bitcast.89, f32[2,64,128]{2,1,0:T(8,128)} %bitcast.90, ...), custom_call_target="tpu_custom_call" | custom-call | tf_op jit(solution)/shard_map/pallas_call | solution.py:324
  129.1 9.1 %shard_map.97 = (f32[1,2,64,256]{3,2,1,0:T(8,128)}, f32[1,2,32,256]{3,2,1,0:T(8,128)}, f32[1,2,64,128]{3,2,1,0:T(8,128)}) custom-call(f32[1,2,64,256]{3,2,1,0:T(8,128)} %bitcast.78, f32[1,2,32,256]{3,2,1,0:T(8,128)} %bitcast.95, f32[1,2,64,128]{3,2,1,0:T(8,128)} %bitcast.96), custom_call_target="tpu_custom_call" | custom-call | tf_op jit(solution)/shard_map/pallas_call | solution.py:271
  138.2 15.7 %shard_map.98 = (f32[32,64,256]{2,1,0:T(8,128)}, f32[32,64,256]{2,1,0:T(8,128)}, f32[2,64,256]{2,1,0:T(8,128)}, f32[2,32,256]{2,1,0:T(8,128)}, f32[2,64,128]{2,1,0:T(8,128)}) custom-call(f32[32,64,256]{2,1,0:T(8,128)} %get-tuple-element.98.lam, f32[2,64,256]{2,1,0:T(8,128)} %bitcast.72, f32[2,32,256]{2,1,0:T(8,128)} %bitcast.83, f32[2,64,128]{2,1,0:T(8,128)} %bitcast.84, ...), custom_call_target="tpu_custom_call" | custom-call | tf_op jit(solution)/shard_map/pallas_call | solution.py:324
  153.9 9.1 %shard_map.99 = (f32[1,2,64,256]{3,2,1,0:T(8,128)}, f32[1,2,32,256]{3,2,1,0:T(8,128)}, f32[1,2,64,128]{3,2,1,0:T(8,128)}) custom-call(f32[1,2,64,256]{3,2,1,0:T(8,128)} %bitcast.76, f32[1,2,32,256]{3,2,1,0:T(8,128)} %bitcast.91, f32[1,2,64,128]{3,2,1,0:T(8,128)} %bitcast.92), custom_call_target="tpu_custom_call" | custom-call | tf_op jit(solution)/shard_map/pallas_call | solution.py:271
  163.0 15.6 %shard_map.100 = (f32[32,64,256]{2,1,0:T(8,128)}, f32[32,64,256]{2,1,0:T(8,128)}, f32[2,64,256]{2,1,0:T(8,128)}, f32[2,32,256]{2,1,0:T(8,128)}, f32[2,64,128]{2,1,0:T(8,128)}) custom-call(f32[32,64,256]{2,1,0:T(8,128)} %get-tuple-element.106.lam, f32[2,64,256]{2,1,0:T(8,128)} %bitcast.73, f32[2,32,256]{2,1,0:T(8,128)} %bitcast.85, f32[2,64,128]{2,1,0:T(8,128)} %bitcast.86, ...), custom_call_target="tpu_custom_call" | custom-call | tf_op jit(solution)/shard_map/pallas_call | solution.py:324
  178.6 9.1 %shard_map.101 = (f32[1,2,64,256]{3,2,1,0:T(8,128)}, f32[1,2,32,256]{3,2,1,0:T(8,128)}, f32[1,2,64,128]{3,2,1,0:T(8,128)}) custom-call(f32[1,2,64,256]{3,2,1,0:T(8,128)} %bitcast.77, f32[1,2,32,256]{3,2,1,0:T(8,128)} %bitcast.93, f32[1,2,64,128]{3,2,1,0:T(8,128)} %bitcast.94), custom_call_target="tpu_custom_call" | custom-call | tf_op jit(solution)/shard_map/pallas_call | solution.py:271
  187.8 14.3 %shard_map.102 = (f32[32,64,256]{2,1,0:T(8,128)}, f32[32,64,256]{2,1,0:T(8,128)}) custom-call(f32[32,64,256]{2,1,0:T(8,128)} %get-tuple-element.114.lam, f32[2,64,256]{2,1,0:T(8,128)} %bitcast.74, f32[2,32,256]{2,1,0:T(8,128)} %bitcast.87, f32[2,64,128]{2,1,0:T(8,128)} %bitcast.88, f32[32,64,256]{2,1,0:T(8,128)} %u.3, f32[2,64,256]{2,1,0:T(8,128)} %get-tuple-element.125.uxh, ...), custom_call_target="tpu_custom_call" | custom-call | tf_op jit(solution)/shard_map/pallas_call | solution.py:324

commit v2 on v0

v2 whole, which is shorter than its diff:
```python
import functools

import jax
import jax.numpy as jnp
from jax import lax
from jax.experimental import pallas as pl
from jax.experimental.pallas import tpu as pltpu
from jax.sharding import PartitionSpec as P

ITERS = 4
MATERIALS = 4

RATE = 0.15
HALF_RATE = 0.5 * RATE
AXES = ("gx", "gy", "gz")
LANES = 128
VMEM_LIMIT = 56 * 1024 * 1024
MESH_ID = pl.DeviceIdType.MESH


def _vmem():
    return pl.BlockSpec(memory_space=pltpu.VMEM)


def _smem():
    return pl.BlockSpec(memory_space=pltpu.SMEM)


class Geo:
    def __init__(self, shape):
        self.X, self.Y, self.Z = shape
        self.row = lax.broadcasted_iota(jnp.int32, (self.Y, self.Z), 0)
        self.lane = lax.broadcasted_iota(jnp.int32, (self.Y, self.Z), 1)
        self.lane128 = lax.broadcasted_iota(jnp.int32, (self.Y, LANES), 1)

    def widen(self, v):
        return jnp.concatenate([v] * (self.Z // LANES), axis=1)


def _slab_nbrs(g, F, halo, x, pos):
    xh, yh, zh = halo
    c = F[x]
    xm = xh[0] if pos == "first" else F[x - 1]
    xp = xh[1] if pos == "last" else F[x + 1]
    ym = jnp.where(g.row == 0, yh[0, pl.ds(x, 1), :], pltpu.roll(c, 1, 0))
    yp = jnp.where(g.row == g.Y - 1, yh[1, pl.ds(x, 1), :], pltpu.roll(c, g.Y - 1, 0))
    zlo = pltpu.roll(zh[0], lax.rem(LANES - x, LANES), 1)
    zhi = pltpu.roll(zh[1], lax.rem(LANES - 1 - x + LANES, LANES), 1)
    zm = jnp.where(g.lane == 0, g.widen(zlo), pltpu.roll(c, 1, 1))
    zp = jnp.where(g.lane == g.Z - 1, g.widen(zhi), pltpu.roll(c, g.Z - 1, 1))
    return c, (xm, xp, ym, yp, zm, zp)


def _pack(g, faces, x, new, pos):
    xs, ys, zs = faces
    if pos == "first":
        xs[0] = new
    if pos == "last":
        xs[1] = new
    ys[0, pl.ds(x, 1), :] = new[0:1, :]
    ys[1, pl.ds(x, 1), :] = new[g.Y - 1 : g.Y, :]
    w0 = pltpu.roll(new[:, 0:LANES], x, 1)
    w1 = pltpu.roll(new[:, g.Z - LANES : g.Z], lax.rem(x + 1, LANES), 1)
    zs[0] = jnp.where(g.lane128 == x, w0, zs[0])
    zs[1] = jnp.where(g.lane128 == x, w1, zs[1])


def _zero_faces(faces):
    zs = faces[2]
    zs[...] = jnp.zeros(zs.shape, zs.dtype)


def _over_slabs(X, body):
    body(0, "first")
    if X > 2:

        def step(x, carry):
            body(x, "mid")
            return carry

        lax.fori_loop(1, X - 1, step, 0)
    body(X - 1, "last")


def _factor(scale, lab):
    f = jnp.where(lab == 2, scale[2], scale[3])
    f = jnp.where(lab == 1, scale[1], f)
    return jnp.where(lab == 0, scale[0], f)


def _stencil(c, nb, kc, knb):
    total = jnp.zeros_like(c)
    for v, k in zip(nb, knb):
        total = total + (kc + k) * (v - c)
    return c + HALF_RATE * total


N_EX = 2 * ITERS + 1


def _window_kernel(
    sizes,
    ckpt, diff, scale, labels, meas, obs, adj,
    grad, lam_out,
    kap, u1, u2, u3, la, lb, xs, ys, zs, xh, yh, zh, send_sem, recv_sem,
):
    g = Geo(ckpt.shape)
    idx = [lax.axis_index(a) for a in AXES]

    def nbr(a, d):
        coords = list(idx)
        coords[a] = idx[a] + d
        return tuple(coords)

    def has(a, d):
        return jnp.logical_and(idx[a] + d >= 0, idx[a] + d < sizes[a])

    zs[...] = jnp.zeros(zs.shape, zs.dtype)
    halos = (xh, yh, zh)
    for a, dst in enumerate(halos):
        for s, d in ((0, -1), (1, 1)):

            @pl.when(jnp.logical_not(has(a, d)))
            def _():
                dst[:, s] = jnp.zeros(dst.shape[:1] + dst.shape[2:], dst.dtype)

    barrier = pltpu.get_barrier_semaphore()
    count = jnp.int32(0)
    for a in range(3):
        for d in (-1, 1):

            @pl.when(has(a, d))
            def _():
                pl.semaphore_signal(barrier, 1, device_id=nbr(a, d), device_id_type=MESH_ID)

            count = count + has(a, d).astype(jnp.int32)
    pl.semaphore_wait(barrier, count)

    sends = (xs, ys, zs)

    def copy(e, a, s):
        k = 2 * a + s
        return pltpu.make_async_remote_copy(
            src_ref=sends[a].at[e, 1 - s],
            dst_ref=halos[a].at[e, s],
            send_sem=send_sem.at[e, k],
            recv_sem=recv_sem.at[e, k],
            device_id=nbr(a, 1 if s == 0 else -1),
            device_id_type=MESH_ID,
        )

    def start(e):
        for a in range(3):
            for s in (0, 1):

                @pl.when(has(a, 1 if s == 0 else -1))
                def _():
                    copy(e, a, s).start()

    def wait(e):
        for a in range(3):
            for s in (0, 1):

                @pl.when(has(a, -1 if s == 0 else 1))
                def _():
                    copy(e, a, s).wait_recv()

                @pl.when(has(a, 1 if s == 0 else -1))
                def _():
                    copy(e, a, s).wait_send()

    def faces(e):
        return (xs.at[e], ys.at[e], zs.at[e])

    def halo(e):
        return (xh.at[e], yh.at[e], zh.at[e])

    def prep(x, pos):
        k = diff[x] * _factor(scale, labels[x])
        kap[x] = k
        _pack(g, faces(0), x, k, pos)
        _pack(g, faces(1), x, ckpt[x], pos)

    _over_slabs(g.X, prep)
    start(0)
    start(1)
    wait(0)
    wait(1)
    kh = halo(0)

    us = (ckpt, u1, u2, u3)
    for n in range(ITERS):
        last = n == ITERS - 1
        src, out = us[n], (la if last else us[n + 1])
        e_in, e_out = 1 + n, 2 + n

        def fwd(x, pos):
            c, nb = _slab_nbrs(g, src, halo(e_in), x, pos)
            kc, knb = _slab_nbrs(g, kap, kh, x, pos)
            new = _stencil(c, nb, kc, knb)
            if last:
                new = adj[x] + obs[x].astype(jnp.float32) * (new - meas[x])
            out[x] = new
            _pack(g, faces(e_out), x, new, pos)

        _over_slabs(g.X, fwd)
        start(e_out)
        wait(e_out)

    lams = (la, lb, la, lb)
    for i, n in enumerate(range(ITERS - 1, -1, -1)):
        first, final = n == ITERS - 1, n == 0
        lam, u = lams[i], us[n]
        e_lam, e_u, e_out = ITERS + 1 + i, 1 + n, ITERS + 2 + i
        out = lam_out if final else lams[i + 1]

        def bwd(x, pos):
            lc, lnb = _slab_nbrs(g, lam, halo(e_lam), x, pos)
            uc, unb = _slab_nbrs(g, u, halo(e_u), x, pos)
            kc, knb = _slab_nbrs(g, kap, kh, x, pos)
            s = jnp.zeros_like(lc)
            t = jnp.zeros_like(lc)
            for lj, uj, kj in zip(lnb, unb, knb):
                d = lj - lc
                s = s + (kc + kj) * d
                t = t + d * (uj - uc)
            new = lc + HALF_RATE * s
            term = (-HALF_RATE) * t
            acc = term if first else grad[x] + term
            if final:
                acc = acc * _factor(scale, labels[x])
            grad[x] = acc
            out[x] = new
            if not final:
                _pack(g, faces(e_out), x, new, pos)

        _over_slabs(g.X, bwd)
        if not final:
            start(e_out)
            wait(e_out)


def _shards(sizes, checkpoint, diffusivity, material_scale, labels, measured, observed, adjoint_in):
    X, Y, Z = checkpoint.shape
    field = jax.ShapeDtypeStruct((X, Y, Z), jnp.float32)
    f32 = jnp.float32
    in_specs = [_vmem(), _vmem(), _smem(), _vmem(), _vmem(), _vmem(), _vmem()]
    return pl.pallas_call(
        functools.partial(_window_kernel, sizes),
        out_shape=(field, field),
        in_specs=in_specs,
        out_specs=(_vmem(), _vmem()),
        scratch_shapes=[pltpu.VMEM((X, Y, Z), f32) for _ in range(6)]
        + [
            pltpu.VMEM((N_EX, 2, Y, Z), f32),
            pltpu.VMEM((N_EX, 2, X, Z), f32),
            pltpu.VMEM((N_EX, 2, Y, LANES), f32),
            pltpu.VMEM((N_EX, 2, Y, Z), f32),
            pltpu.VMEM((N_EX, 2, X, Z), f32),
            pltpu.VMEM((N_EX, 2, Y, LANES), f32),
            pltpu.SemaphoreType.DMA((N_EX, 6)),
            pltpu.SemaphoreType.DMA((N_EX, 6)),
        ],
        compiler_params=pltpu.CompilerParams(
            vmem_limit_bytes=VMEM_LIMIT, collective_id=0, has_side_effects=True
        ),
    )(checkpoint, diffusivity, material_scale, labels, measured, observed, adjoint_in)


def solution(mesh):
    sizes = tuple(mesh.shape[a] for a in AXES)
    block = P("gx", "gy", "gz")
    placed = (block, block, P(), block, block, block, block)
    return jax.shard_map(
        functools.partial(_shards, sizes),
        mesh=mesh,
        in_specs=placed,
        out_specs=(block, block),
        check_vma=False,
    )
```

time: 545 us -> 135 us (0.25)
  the two profiles are of different devices: /device:TPU:113 before, /device:TPU:0 now
where the time goes in v2:
time: 135 us
  Pallas kernels  129 us (96%)
  local copies, waits for them, and re-layouts  4.6 us (3%)
    pallas_call x1, Pallas kernels, _shards(): pl.pallas_call(functools.partial(_window_kernel, sizes), out_shape=(field...  129 us
    unnamed x4, local copies, waits for them, and re-layouts  4.6 us

profile of v2, /device:TPU:0, one launch (start us, length us, event | category | flops | bytes accessed | tf_op | source)
XLA Modules:
  0.0 134.7 jit_solution(6305636793130216434)
XLA Ops:
  0.6 129.5 %shard_map.86 = (f32[32,64,256]{2,1,0:T(8,128)}, f32[32,64,256]{2,1,0:T(8,128)}) custom-call(f32[32,64,256]{2,1,0:T(8,128)} %ckpt.1, f32[32,64,256]{2,1,0:T(8,128)} %diff.1, f32[4]{0:T(128)} %scale.1, s32[32,64,256]{2,1,0:T(8,128)} %labels.1, f32[32,64,256]{2,1,0:T(8,128)} %meas.1, s32[32,64,256]{2,1,0:T(8,128)} %obs.1, f32[32,64,256]{2,1,0:T(8,128)} %adj.1), custom_call_target="tpu_custom_call" | custom-call | tf_op jit(solution)/shard_map/pallas_call | solution.py:248
  130.1 0.0 copy-start
  130.1 3.3 %copy.11 = f32[32,64,256]{2,1,0:T(8,128)} copy(f32[32,64,256]{2,1,0:T(8,128)} %get-tuple-element.4) | data formatting | bytes 4194304
  133.4 0.0 copy-done
  133.4 1.3 copy.12
Async XLA Ops:
  130.1 3.3 %copy-start = (f32[32,64,256]{2,1,0:T(8,128)S(1)}, f32[32,64,256]{2,1,0:T(8,128)}, u32[]{:S(2)}) copy-start(f32[32,64,256]{2,1,0:T(8,128)} %get-tuple-element.5) | copy-start | bytes 6291460

commit v3 on v2

--- a/solution.py
+++ b/solution.py
@@ -32,6 +32,7 @@
         self.row = lax.broadcasted_iota(jnp.int32, (self.Y, self.Z), 0)
         self.lane = lax.broadcasted_iota(jnp.int32, (self.Y, self.Z), 1)
         self.lane128 = lax.broadcasted_iota(jnp.int32, (self.Y, LANES), 1)
+        self.row8 = lax.broadcasted_iota(jnp.int32, (8, self.Z), 0)
 
     def widen(self, v):
         return jnp.concatenate([v] * (self.Z // LANES), axis=1)
@@ -39,15 +40,22 @@
 
 def _slab_nbrs(g, F, halo, x, pos):
     xh, yh, zh = halo
+    Y, Z = g.Y, g.Z
     c = F[x]
     xm = xh[0] if pos == "first" else F[x - 1]
     xp = xh[1] if pos == "last" else F[x + 1]
-    ym = jnp.where(g.row == 0, yh[0, pl.ds(x, 1), :], pltpu.roll(c, 1, 0))
-    yp = jnp.where(g.row == g.Y - 1, yh[1, pl.ds(x, 1), :], pltpu.roll(c, g.Y - 1, 0))
+    ym = pltpu.roll(c, 1, 0)
+    ym = jnp.concatenate([jnp.where(g.row8 == 0, yh[0, pl.ds(x, 1), :], ym[0:8]), ym[8:]], axis=0)
+    yp = pltpu.roll(c, Y - 1, 0)
+    yp = jnp.concatenate([yp[: Y - 8], jnp.where(g.row8 == 7, yh[1, pl.ds(x, 1), :], yp[Y - 8 :])], axis=0)
     zlo = pltpu.roll(zh[0], lax.rem(LANES - x, LANES), 1)
     zhi = pltpu.roll(zh[1], lax.rem(LANES - 1 - x + LANES, LANES), 1)
-    zm = jnp.where(g.lane == 0, g.widen(zlo), pltpu.roll(c, 1, 1))
-    zp = jnp.where(g.lane == g.Z - 1, g.widen(zhi), pltpu.roll(c, g.Z - 1, 1))
+    zm = pltpu.roll(c, 1, 1)
+    zm = jnp.concatenate([jnp.where(g.lane128 == 0, zlo, zm[:, 0:LANES]), zm[:, LANES:]], axis=1)
+    zp = pltpu.roll(c, Z - 1, 1)
+    zp = jnp.concatenate(
+        [zp[:, : Z - LANES], jnp.where(g.lane128 == LANES - 1, zhi, zp[:, Z - LANES :])], axis=1
+    )
     return c, (xm, xp, ym, yp, zm, zp)
 
 
@@ -88,10 +96,10 @@
     return jnp.where(lab == 0, scale[0], f)
 
 
-def _stencil(c, nb, kc, knb):
+def _stencil(c, nb, conds):
     total = jnp.zeros_like(c)
-    for v, k in zip(nb, knb):
-        total = total + (kc + k) * (v - c)
+    for v, k in zip(nb, conds):
+        total = total + k * (v - c)
     return c + HALF_RATE * total
 
 
@@ -102,7 +110,7 @@
     sizes,
     ckpt, diff, scale, labels, meas, obs, adj,
     grad, lam_out,
-    kap, u1, u2, u3, la, lb, xs, ys, zs, xh, yh, zh, send_sem, recv_sem,
+    kap, cond, u1, u2, u3, la, lb, xs, ys, zs, xh, yh, zh, send_sem, recv_sem,
 ):
     g = Geo(ckpt.shape)
     idx = [lax.axis_index(a) for a in AXES]
@@ -185,8 +193,14 @@
     start(0)
     start(1)
     wait(0)
+
+    def conduct(x, pos):
+        kc, knb = _slab_nbrs(g, kap, halo(0), x, pos)
+        for j, kj in enumerate(knb):
+            cond[j, x] = kc + kj
+
+    _over_slabs(g.X, conduct)
     wait(1)
-    kh = halo(0)
 
     us = (ckpt, u1, u2, u3)
     for n in range(ITERS):
@@ -196,8 +210,7 @@
 
         def fwd(x, pos):
             c, nb = _slab_nbrs(g, src, halo(e_in), x, pos)
-            kc, knb = _slab_nbrs(g, kap, kh, x, pos)
-            new = _stencil(c, nb, kc, knb)
+            new = _stencil(c, nb, [cond[j, x] for j in range(6)])
             if last:
                 new = adj[x] + obs[x].astype(jnp.float32) * (new - meas[x])
             out[x] = new
@@ -217,12 +230,11 @@
         def bwd(x, pos):
             lc, lnb = _slab_nbrs(g, lam, halo(e_lam), x, pos)
             uc, unb = _slab_nbrs(g, u, halo(e_u), x, pos)
-            kc, knb = _slab_nbrs(g, kap, kh, x, pos)
             s = jnp.zeros_like(lc)
             t = jnp.zeros_like(lc)
-            for lj, uj, kj in zip(lnb, unb, knb):
+            for j, (lj, uj) in enumerate(zip(lnb, unb)):
                 d = lj - lc
-                s = s + (kc + kj) * d
+                s = s + cond[j, x] * d
                 t = t + d * (uj - uc)
             new = lc + HALF_RATE * s
             term = (-HALF_RATE) * t
@@ -250,7 +262,8 @@
         out_shape=(field, field),
         in_specs=in_specs,
         out_specs=(_vmem(), _vmem()),
-        scratch_shapes=[pltpu.VMEM((X, Y, Z), f32) for _ in range(6)]
+        scratch_shapes=[pltpu.VMEM((X, Y, Z), f32), pltpu.VMEM((6, X, Y, Z), f32)]
+        + [pltpu.VMEM((X, Y, Z), f32) for _ in range(5)]
         + [
             pltpu.VMEM((N_EX, 2, Y, Z), f32),
             pltpu.VMEM((N_EX, 2, X, Z), f32),

time: 135 us -> 120 us (0.89)
  Pallas kernels: 129 us -> 114 us
    pallas_call x1, Pallas kernels: 129 us -> 114 us  [_shards(): pl.pallas_call(functools.partial(_window_kernel, sizes), out_shape=(field...]
where the time goes in v3:
time: 120 us
  Pallas kernels  114 us (95%)
  local copies, waits for them, and re-layouts  4.6 us (4%)
    pallas_call x1, Pallas kernels, _shards(): pl.pallas_call(functools.partial(_window_kernel, sizes), out_shape=(field...  114 us
    unnamed x4, local copies, waits for them, and re-layouts  4.6 us

profile of v3, /device:TPU:0, one launch (start us, length us, event | category | flops | bytes accessed | tf_op | source)
XLA Modules:
  0.0 119.7 jit_solution(8947631389726804472)
XLA Ops:
  0.6 114.5 %shard_map.86 = (f32[32,64,256]{2,1,0:T(8,128)}, f32[32,64,256]{2,1,0:T(8,128)}) custom-call(f32[32,64,256]{2,1,0:T(8,128)} %ckpt.1, f32[32,64,256]{2,1,0:T(8,128)} %diff.1, f32[4]{0:T(128)} %scale.1, s32[32,64,256]{2,1,0:T(8,128)} %labels.1, f32[32,64,256]{2,1,0:T(8,128)} %meas.1, s32[32,64,256]{2,1,0:T(8,128)} %obs.1, f32[32,64,256]{2,1,0:T(8,128)} %adj.1), custom_call_target="tpu_custom_call" | custom-call | tf_op jit(solution)/shard_map/pallas_call | solution.py:260
  115.1 0.0 copy-start
  115.1 3.3 %copy.11 = f32[32,64,256]{2,1,0:T(8,128)} copy(f32[32,64,256]{2,1,0:T(8,128)} %get-tuple-element.4) | data formatting | bytes 4194304
  118.4 0.0 copy-done
  118.4 1.3 %copy.12 = f32[32,64,256]{2,1,0:T(8,128)} copy(f32[32,64,256]{2,1,0:T(8,128)S(1)} %copy-done) | data formatting | bytes 4194304
Async XLA Ops:
  115.1 3.3 %copy-start = (f32[32,64,256]{2,1,0:T(8,128)S(1)}, f32[32,64,256]{2,1,0:T(8,128)}, u32[]{:S(2)}) copy-start(f32[32,64,256]{2,1,0:T(8,128)} %get-tuple-element.5) | copy-start | bytes 6291460

commit v4 on v3

--- a/solution.py
+++ b/solution.py
@@ -59,6 +59,47 @@
     return c, (xm, xp, ym, yp, zm, zp)
 
 
+def _local_nbrs(g, F, x, pos):
+    Y, Z = g.Y, g.Z
+    c = F[x]
+    xm = c if pos == "first" else F[x - 1]
+    xp = c if pos == "last" else F[x + 1]
+    ym = pltpu.roll(c, 1, 0)
+    ym = jnp.concatenate([jnp.where(g.row8 == 0, c[0:8], ym[0:8]), ym[8:]], axis=0)
+    yp = pltpu.roll(c, Y - 1, 0)
+    yp = jnp.concatenate([yp[: Y - 8], jnp.where(g.row8 == 7, c[Y - 8 :], yp[Y - 8 :])], axis=0)
+    zm = pltpu.roll(c, 1, 1)
+    zm = jnp.concatenate([jnp.where(g.lane128 == 0, c[:, 0:LANES], zm[:, 0:LANES]), zm[:, LANES:]], axis=1)
+    zp = pltpu.roll(c, Z - 1, 1)
+    zp = jnp.concatenate(
+        [zp[:, : Z - LANES], jnp.where(g.lane128 == LANES - 1, c[:, Z - LANES :], zp[:, Z - LANES :])],
+        axis=1,
+    )
+    return c, (xm, xp, ym, yp, zm, zp)
+
+
+def _edges(g, halo, x, pos):
+    xh, yh, zh = halo
+    Y, Z = g.Y, g.Z
+    full = (slice(None), slice(None))
+    out = []
+    if pos == "first":
+        out.append((0, full, None, xh[0]))
+    if pos == "last":
+        out.append((1, full, None, xh[1]))
+    out.append((2, (slice(0, 8), slice(None)), g.row8 == 0, yh[0, pl.ds(x, 1), :]))
+    out.append((3, (slice(Y - 8, Y), slice(None)), g.row8 == 7, yh[1, pl.ds(x, 1), :]))
+    zlo = pltpu.roll(zh[0], lax.rem(LANES - x, LANES), 1)
+    zhi = pltpu.roll(zh[1], lax.rem(LANES - 1 - x + LANES, LANES), 1)
+    out.append((4, (slice(None), slice(0, LANES)), g.lane128 == 0, zlo))
+    out.append((5, (slice(None), slice(Z - LANES, Z)), g.lane128 == LANES - 1, zhi))
+    return out
+
+
+def _masked(mask, v):
+    return v if mask is None else jnp.where(mask, v, 0.0)
+
+
 def _pack(g, faces, x, new, pos):
     xs, ys, zs = faces
     if pos == "first":
@@ -200,7 +241,6 @@
             cond[j, x] = kc + kj
 
     _over_slabs(g.X, conduct)
-    wait(1)
 
     us = (ckpt, u1, u2, u3)
     for n in range(ITERS):
@@ -208,17 +248,25 @@
         src, out = us[n], (la if last else us[n + 1])
         e_in, e_out = 1 + n, 2 + n
 
-        def fwd(x, pos):
-            c, nb = _slab_nbrs(g, src, halo(e_in), x, pos)
-            new = _stencil(c, nb, [cond[j, x] for j in range(6)])
+        def fwd_inner(x, pos):
+            c, nb = _local_nbrs(g, src, x, pos)
+            out[x] = _stencil(c, nb, [cond[j, x] for j in range(6)])
+
+        def fwd_edge(x, pos):
+            for j, tile, mask, h in _edges(g, halo(e_in), x, pos):
+                cc = src.at[x][tile]
+                delta = _masked(mask, cond.at[j, x][tile] * (h - cc))
+                out.at[x][tile] = out.at[x][tile] + HALF_RATE * delta
+            new = out[x]
             if last:
                 new = adj[x] + obs[x].astype(jnp.float32) * (new - meas[x])
-            out[x] = new
+                out[x] = new
             _pack(g, faces(e_out), x, new, pos)
 
-        _over_slabs(g.X, fwd)
+        _over_slabs(g.X, fwd_inner)
+        wait(e_in)
+        _over_slabs(g.X, fwd_edge)
         start(e_out)
-        wait(e_out)
 
     lams = (la, lb, la, lb)
     for i, n in enumerate(range(ITERS - 1, -1, -1)):
@@ -227,29 +275,38 @@
         e_lam, e_u, e_out = ITERS + 1 + i, 1 + n, ITERS + 2 + i
         out = lam_out if final else lams[i + 1]
 
-        def bwd(x, pos):
-            lc, lnb = _slab_nbrs(g, lam, halo(e_lam), x, pos)
-            uc, unb = _slab_nbrs(g, u, halo(e_u), x, pos)
+        def bwd_inner(x, pos):
+            lc, lnb = _local_nbrs(g, lam, x, pos)
+            uc, unb = _local_nbrs(g, u, x, pos)
             s = jnp.zeros_like(lc)
             t = jnp.zeros_like(lc)
             for j, (lj, uj) in enumerate(zip(lnb, unb)):
                 d = lj - lc
                 s = s + cond[j, x] * d
                 t = t + d * (uj - uc)
-            new = lc + HALF_RATE * s
+            out[x] = lc + HALF_RATE * s
             term = (-HALF_RATE) * t
-            acc = term if first else grad[x] + term
+            grad[x] = term if first else grad[x] + term
+
+        def bwd_edge(x, pos):
+            lam_edges = _edges(g, halo(e_lam), x, pos)
+            u_edges = _edges(g, halo(e_u), x, pos)
+            for (j, tile, mask, hl), (_, _, _, hu) in zip(lam_edges, u_edges):
+                d = hl - lam.at[x][tile]
+                ds = _masked(mask, cond.at[j, x][tile] * d)
+                dt = _masked(mask, d * (hu - u.at[x][tile]))
+                out.at[x][tile] = out.at[x][tile] + HALF_RATE * ds
+                grad.at[x][tile] = grad.at[x][tile] + (-HALF_RATE) * dt
             if final:
-                acc = acc * _factor(scale, labels[x])
-            grad[x] = acc
-            out[x] = new
-            if not final:
-                _pack(g, faces(e_out), x, new, pos)
-
-        _over_slabs(g.X, bwd)
+                grad[x] = grad[x] * _factor(scale, labels[x])
+            else:
+                _pack(g, faces(e_out), x, out[x], pos)
+
+        _over_slabs(g.X, bwd_inner)
+        wait(e_lam)
+        _over_slabs(g.X, bwd_edge)
         if not final:
             start(e_out)
-            wait(e_out)
 
 
 def _shards(sizes, checkpoint, diffusivity, material_scale, labels, measured, observed, adjoint_in):

time: 120 us -> 111 us (0.925)
  Pallas kernels: 114 us -> 106 us
    pallas_call x1, Pallas kernels: 114 us -> 106 us  [_shards(): pl.pallas_call(functools.partial(_window_kernel, sizes), out_shape=(field...]
where the time goes in v4:
time: 111 us
  Pallas kernels  106 us (95%)
  local copies, waits for them, and re-layouts  4.6 us (4%)
    pallas_call x1, Pallas kernels, _shards(): pl.pallas_call(functools.partial(_window_kernel, sizes), out_shape=(field...  106 us
    unnamed x4, local copies, waits for them, and re-layouts  4.6 us

profile of v4, /device:TPU:0, one launch (start us, length us, event | category | flops | bytes accessed | tf_op | source)
XLA Modules:
  0.0 111.1 jit_solution(4340590050630617871)
XLA Ops:
  0.6 105.8 %shard_map.86 = (f32[32,64,256]{2,1,0:T(8,128)}, f32[32,64,256]{2,1,0:T(8,128)}) custom-call(f32[32,64,256]{2,1,0:T(8,128)} %ckpt.1, f32[32,64,256]{2,1,0:T(8,128)} %diff.1, f32[4]{0:T(128)} %scale.1, s32[32,64,256]{2,1,0:T(8,128)} %labels.1, f32[32,64,256]{2,1,0:T(8,128)} %meas.1, s32[32,64,256]{2,1,0:T(8,128)} %obs.1, f32[32,64,256]{2,1,0:T(8,128)} %adj.1), custom_call_target="tpu_custom_call" | custom-call | tf_op jit(solution)/shard_map/pallas_call | solution.py:317
  106.5 0.0 copy-start
  106.5 3.3 %copy.11 = f32[32,64,256]{2,1,0:T(8,128)} copy(f32[32,64,256]{2,1,0:T(8,128)} %get-tuple-element.4) | data formatting | bytes 4194304
  109.8 0.0 copy-done
  109.8 1.3 %copy.12 = f32[32,64,256]{2,1,0:T(8,128)} copy(f32[32,64,256]{2,1,0:T(8,128)S(1)} %copy-done) | data formatting | bytes 4194304
Async XLA Ops:
  106.5 3.3 %copy-start = (f32[32,64,256]{2,1,0:T(8,128)S(1)}, f32[32,64,256]{2,1,0:T(8,128)}, u32[]{:S(2)}) copy-start(f32[32,64,256]{2,1,0:T(8,128)} %get-tuple-element.5) | copy-start | bytes 6291460

commit v5 on v3

v5 whole, which is shorter than its diff:
```python
import functools

import jax
import jax.numpy as jnp
from jax import lax
from jax.experimental import pallas as pl
from jax.experimental.pallas import tpu as pltpu
from jax.sharding import PartitionSpec as P

ITERS = 4
MATERIALS = 4

RATE = 0.15
HALF_RATE = 0.5 * RATE
AXES = ("gx", "gy", "gz")
LANES = 128
VMEM_LIMIT = 56 * 1024 * 1024
MESH_ID = pl.DeviceIdType.MESH


def _vmem():
    return pl.BlockSpec(memory_space=pltpu.VMEM)


def _smem():
    return pl.BlockSpec(memory_space=pltpu.SMEM)


class Geo:
    def __init__(self, shape):
        self.X, self.Y, self.Z = shape
        self.row = lax.broadcasted_iota(jnp.int32, (self.Y, self.Z), 0)
        self.lane = lax.broadcasted_iota(jnp.int32, (self.Y, self.Z), 1)
        self.lane128 = lax.broadcasted_iota(jnp.int32, (self.Y, LANES), 1)
        self.row8 = lax.broadcasted_iota(jnp.int32, (8, self.Z), 0)

    def widen(self, v):
        return jnp.concatenate([v] * (self.Z // LANES), axis=1)


def _slab_nbrs(g, F, halo, x, pos, zl):
    xh, yh, zh = halo
    Y, Z = g.Y, g.Z
    c = F[x]
    xm = xh[0] if pos == "first" else F[x - 1]
    xp = xh[1] if pos == "last" else F[x + 1]
    ym = pltpu.roll(c, 1, 0)
    ym = jnp.concatenate([jnp.where(g.row8 == 0, yh[0, pl.ds(x, 1), :], ym[0:8]), ym[8:]], axis=0)
    yp = pltpu.roll(c, Y - 1, 0)
    yp = jnp.concatenate([yp[: Y - 8], jnp.where(g.row8 == 7, yh[1, pl.ds(x, 1), :], yp[Y - 8 :])], axis=0)
    zlo = pltpu.roll(zh[0], lax.rem(LANES - zl, LANES), 1)
    zhi = pltpu.roll(zh[1], lax.rem(LANES - 1 - zl + LANES, LANES), 1)
    zm = pltpu.roll(c, 1, 1)
    zm = jnp.concatenate([jnp.where(g.lane128 == 0, zlo, zm[:, 0:LANES]), zm[:, LANES:]], axis=1)
    zp = pltpu.roll(c, Z - 1, 1)
    zp = jnp.concatenate(
        [zp[:, : Z - LANES], jnp.where(g.lane128 == LANES - 1, zhi, zp[:, Z - LANES :])], axis=1
    )
    return c, (xm, xp, ym, yp, zm, zp)


def _pack(g, faces, x, new, pos, zl, zc):
    xs, ys = faces
    if pos == "first":
        xs[0] = new
    if pos == "last":
        xs[1] = new
    ys[0, pl.ds(x, 1), :] = new[0:1, :]
    ys[1, pl.ds(x, 1), :] = new[g.Y - 1 : g.Y, :]
    w0 = pltpu.roll(new[:, 0:LANES], zl, 1)
    w1 = pltpu.roll(new[:, g.Z - LANES : g.Z], lax.rem(zl + 1, LANES), 1)
    z0, z1 = zc
    return (jnp.where(g.lane128 == zl, w0, z0), jnp.where(g.lane128 == zl, w1, z1))


def _half(X, h, body, carry):
    H = X // 2
    if h == 0:
        if H > 1:
            carry = lax.fori_loop(1, H, lambda x, c: body(x, "mid", x, c), carry)
        return body(0, "first", 0, carry)
    if X - 1 > H:
        carry = lax.fori_loop(H, X - 1, lambda x, c: body(x, "mid", x - H, c), carry)
    return body(X - 1, "last", X - 1 - H, carry)


def _factor(scale, lab):
    f = jnp.where(lab == 2, scale[2], scale[3])
    f = jnp.where(lab == 1, scale[1], f)
    return jnp.where(lab == 0, scale[0], f)


def _stencil(c, nb, conds):
    total = jnp.zeros_like(c)
    for v, k in zip(nb, conds):
        total = total + k * (v - c)
    return c + HALF_RATE * total


N_EX = 2 * ITERS + 1
N_COPY = 10


def _window_kernel(
    sizes,
    ckpt, diff, scale, labels, meas, obs, adj,
    grad, lam_out,
    kap, cond, u1, u2, u3, la, lb, xs, ys, zs, xh, yh, zh, send_sem, recv_sem,
):
    g = Geo(ckpt.shape)
    X = g.X
    idx = [lax.axis_index(a) for a in AXES]

    def nbr(a, d):
        coords = list(idx)
        coords[a] = idx[a] + d
        return tuple(coords)

    def has(a, d):
        return jnp.logical_and(idx[a] + d >= 0, idx[a] + d < sizes[a])

    for a, dst in enumerate((xh, yh)):
        for s, d in ((0, -1), (1, 1)):

            @pl.when(jnp.logical_not(has(a, d)))
            def _():
                dst[:, s] = jnp.zeros(dst.shape[:1] + dst.shape[2:], dst.dtype)

    for s, d in ((0, -1), (1, 1)):

        @pl.when(jnp.logical_not(has(2, d)))
        def _():
            zh[:, :, s] = jnp.zeros(zh.shape[:2] + zh.shape[3:], zh.dtype)

    barrier = pltpu.get_barrier_semaphore()
    count = jnp.int32(0)
    for a in range(3):
        for d in (-1, 1):

            @pl.when(has(a, d))
            def _():
                pl.semaphore_signal(barrier, 1, device_id=nbr(a, d), device_id_type=MESH_ID)

            count = count + has(a, d).astype(jnp.int32)
    pl.semaphore_wait(barrier, count)

    H = X // 2

    def copy(e, k):
        if k < 2:
            a, s, src, dst = 0, k, xs.at[e, 1 - k], xh.at[e, k]
        elif k < 6:
            h, s = divmod(k - 2, 2)
            rows = pl.ds(h * H, H) if h == 0 else pl.ds(H, X - H)
            a, src, dst = 1, ys.at[e, 1 - s, rows], yh.at[e, s, rows]
        else:
            h, s = divmod(k - 6, 2)
            a, src, dst = 2, zs.at[e, h, 1 - s], zh.at[e, h, s]
        d = 1 if s == 0 else -1
        desc = pltpu.make_async_remote_copy(
            src_ref=src,
            dst_ref=dst,
            send_sem=send_sem.at[e, k],
            recv_sem=recv_sem.at[e, k],
            device_id=nbr(a, d),
            device_id_type=MESH_ID,
        )
        return desc, a, d

    def start(e, ks):
        for k in ks:
            desc, a, d = copy(e, k)

            @pl.when(has(a, d))
            def _():
                desc.start()

    def wait_recv(e, ks):
        for k in ks:
            desc, a, d = copy(e, k)

            @pl.when(has(a, -d))
            def _():
                desc.wait_recv()

    def wait_send(e, ks):
        for k in ks:
            desc, a, d = copy(e, k)

            @pl.when(has(a, d))
            def _():
                desc.wait_send()

    SENT = ((1, 2, 3, 6, 7), (0, 4, 5, 8, 9))
    NEED = ((2, 3, 6, 7), (1, 4, 5, 8, 9))

    def faces(e):
        return (xs.at[e], ys.at[e])

    def halo(e, h):
        return (xh.at[e], yh.at[e], zh.at[e, h])

    def zero_z():
        z = jnp.zeros((g.Y, LANES), jnp.float32)
        return (z, z)

    def store_z(e, h, zc):
        zs[e, h, 0] = zc[0]
        zs[e, h, 1] = zc[1]

    def sweep(e_in, e_out, body):
        for h in (0, 1):
            if e_in is not None:
                wait_recv(e_in, NEED[h])
                if h == 1:
                    wait_send(e_in, range(N_COPY))

            def run(x, pos, zl, zc):
                if pos == "first" and e_in is not None:
                    wait_recv(e_in, (0,))
                return body(x, pos, zl, zc, h)

            zc = _half(X, h, run, zero_z())
            if e_out is not None:
                store_z(e_out, h, zc)
                start(e_out, SENT[h])

    def prep(x, pos, zl, zc, h):
        k = diff[x] * _factor(scale, labels[x])
        kap[x] = k
        zk, zu = zc
        zk = _pack(g, faces(0), x, k, pos, zl, zk)
        zu = _pack(g, faces(1), x, ckpt[x], pos, zl, zu)
        return (zk, zu)

    for h in (0, 1):
        zc = _half(X, h, lambda x, pos, zl, zc: prep(x, pos, zl, zc, h), (zero_z(), zero_z()))
        store_z(0, h, zc[0])
        store_z(1, h, zc[1])
        start(0, SENT[h])
        start(1, SENT[h])

    def conduct(x, pos, zl, zc, h):
        kc, knb = _slab_nbrs(g, kap, halo(0, h), x, pos, zl)
        for j, kj in enumerate(knb):
            cond[j, x] = kc + kj
        return zc

    sweep(0, None, conduct)

    us = (ckpt, u1, u2, u3)
    for n in range(ITERS):
        last = n == ITERS - 1
        src, out = us[n], (la if last else us[n + 1])
        e_in, e_out = 1 + n, 2 + n

        def fwd(x, pos, zl, zc, h):
            c, nb = _slab_nbrs(g, src, halo(e_in, h), x, pos, zl)
            new = _stencil(c, nb, [cond[j, x] for j in range(6)])
            if last:
                new = adj[x] + obs[x].astype(jnp.float32) * (new - meas[x])
            out[x] = new
            return _pack(g, faces(e_out), x, new, pos, zl, zc)

        sweep(e_in, e_out, fwd)

    lams = (la, lb, la, lb)
    for i, n in enumerate(range(ITERS - 1, -1, -1)):
        first, final = n == ITERS - 1, n == 0
        lam, u = lams[i], us[n]
        e_lam, e_u, e_out = ITERS + 1 + i, 1 + n, ITERS + 2 + i
        out = lam_out if final else lams[i + 1]

        def bwd(x, pos, zl, zc, h):
            lc, lnb = _slab_nbrs(g, lam, halo(e_lam, h), x, pos, zl)
            uc, unb = _slab_nbrs(g, u, halo(e_u, h), x, pos, zl)
            s = jnp.zeros_like(lc)
            t = jnp.zeros_like(lc)
            for j, (lj, uj) in enumerate(zip(lnb, unb)):
                d = lj - lc
                s = s + cond[j, x] * d
                t = t + d * (uj - uc)
            new = lc + HALF_RATE * s
            term = (-HALF_RATE) * t
            acc = term if first else grad[x] + term
            if final:
                acc = acc * _factor(scale, labels[x])
            grad[x] = acc
            out[x] = new
            if final:
                return zc
            return _pack(g, faces(e_out), x, new, pos, zl, zc)

        sweep(e_lam, None if final else e_out, bwd)


def _shards(sizes, checkpoint, diffusivity, material_scale, labels, measured, observed, adjoint_in):
    X, Y, Z = checkpoint.shape
    field = jax.ShapeDtypeStruct((X, Y, Z), jnp.float32)
    f32 = jnp.float32
    in_specs = [_vmem(), _vmem(), _smem(), _vmem(), _vmem(), _vmem(), _vmem()]
    return pl.pallas_call(
        functools.partial(_window_kernel, sizes),
        out_shape=(field, field),
        in_specs=in_specs,
        out_specs=(_vmem(), _vmem()),
        scratch_shapes=[pltpu.VMEM((X, Y, Z), f32), pltpu.VMEM((6, X, Y, Z), f32)]
        + [pltpu.VMEM((X, Y, Z), f32) for _ in range(5)]
        + [
            pltpu.VMEM((N_EX, 2, Y, Z), f32),
            pltpu.VMEM((N_EX, 2, X, Z), f32),
            pltpu.VMEM((N_EX, 2, 2, Y, LANES), f32),
            pltpu.VMEM((N_EX, 2, Y, Z), f32),
            pltpu.VMEM((N_EX, 2, X, Z), f32),
            pltpu.VMEM((N_EX, 2, 2, Y, LANES), f32),
            pltpu.SemaphoreType.DMA((N_EX, N_COPY)),
            pltpu.SemaphoreType.DMA((N_EX, N_COPY)),
        ],
        compiler_params=pltpu.CompilerParams(
            vmem_limit_bytes=VMEM_LIMIT, collective_id=0, has_side_effects=True
        ),
    )(checkpoint, diffusivity, material_scale, labels, measured, observed, adjoint_in)


def solution(mesh):
    sizes = tuple(mesh.shape[a] for a in AXES)
    block = P("gx", "gy", "gz")
    placed = (block, block, P(), block, block, block, block)
    return jax.shard_map(
        functools.partial(_shards, sizes),
        mesh=mesh,
        in_specs=placed,
        out_specs=(block, block),
        check_vma=False,
    )
```

time: 120 us -> 86.9 us (0.72)
  the two profiles are of different devices: /device:TPU:0 before, /device:TPU:99 now
where the time goes in v5:
time: 86.9 us; the launch traced here: 86.8 us
  Pallas kernels  81.6 us (94%)
  local copies, waits for them, and re-layouts  4.6 us (5%)
    pallas_call x1, Pallas kernels, _shards(): pl.pallas_call(functools.partial(_window_kernel, sizes), out_shape=(field...  81.6 us
    unnamed x4, local copies, waits for them, and re-layouts  4.6 us

profile of v5, /device:TPU:99, one launch (start us, length us, event | category | flops | bytes accessed | tf_op | source)
XLA Modules:
  0.0 86.8 jit_solution(15975127900964766651)
XLA Ops:
  0.6 81.6 %shard_map.86 = (f32[32,64,256]{2,1,0:T(8,128)}, f32[32,64,256]{2,1,0:T(8,128)}) custom-call(f32[32,64,256]{2,1,0:T(8,128)} %ckpt.1, f32[32,64,256]{2,1,0:T(8,128)} %diff.1, f32[4]{0:T(128)} %scale.1, s32[32,64,256]{2,1,0:T(8,128)} %labels.1, f32[32,64,256]{2,1,0:T(8,128)} %meas.1, s32[32,64,256]{2,1,0:T(8,128)} %obs.1, f32[32,64,256]{2,1,0:T(8,128)} %adj.1), custom_call_target="tpu_custom_call" | custom-call | tf_op jit(solution)/shard_map/pallas_call | solution.py:302
  82.2 0.0 copy-start
  82.2 3.3 %copy.11 = f32[32,64,256]{2,1,0:T(8,128)} copy(f32[32,64,256]{2,1,0:T(8,128)} %get-tuple-element.4) | data formatting | bytes 4194304
  85.5 0.0 copy-done
  85.5 1.3 %copy.12 = f32[32,64,256]{2,1,0:T(8,128)} copy(f32[32,64,256]{2,1,0:T(8,128)S(1)} %copy-done) | data formatting | bytes 4194304
Async XLA Ops:
  82.2 3.3 %copy-start = (f32[32,64,256]{2,1,0:T(8,128)S(1)}, f32[32,64,256]{2,1,0:T(8,128)}, u32[]{:S(2)}) copy-start(f32[32,64,256]{2,1,0:T(8,128)} %get-tuple-element.5) | copy-start | bytes 6291460

commit v6 on v5

--- a/solution.py
+++ b/solution.py
@@ -103,12 +103,32 @@
 
 def _window_kernel(
     sizes,
-    ckpt, diff, scale, labels, meas, obs, adj,
+    ckpt_hbm, diff_hbm, scale, labels_hbm, meas_hbm, obs_hbm, adj_hbm,
     grad, lam_out,
-    kap, cond, u1, u2, u3, la, lb, xs, ys, zs, xh, yh, zh, send_sem, recv_sem,
+    ckpt, diff, labels, meas, obs, adj,
+    kap, cond, u1, u2, u3, la, lb, xs, ys, zs, xh, yh, zh, send_sem, recv_sem, load_sem,
 ):
     g = Geo(ckpt.shape)
     X = g.X
+    H = X // 2
+    halves = (pl.ds(0, H), pl.ds(H, X - H))
+    early = ((ckpt_hbm, ckpt), (diff_hbm, diff), (labels_hbm, labels))
+    late = ((meas_hbm, meas), (obs_hbm, obs), (adj_hbm, adj))
+
+    def load(i, src, dst, rows=None):
+        if rows is not None:
+            src, dst = src.at[rows], dst.at[rows]
+        return pltpu.make_async_copy(src, dst, load_sem.at[i])
+
+    def early_load(h, i):
+        src, dst = early[i]
+        return load(2 * i + h, src, dst, halves[h])
+
+    for h in (0, 1):
+        for i in range(3):
+            early_load(h, i).start()
+    for i, (src, dst) in enumerate(late):
+        load(6 + i, src, dst).start()
     idx = [lax.axis_index(a) for a in AXES]
 
     def nbr(a, d):
@@ -143,8 +163,6 @@
 
             count = count + has(a, d).astype(jnp.int32)
     pl.semaphore_wait(barrier, count)
-
-    H = X // 2
 
     def copy(e, k):
         if k < 2:
@@ -234,6 +252,8 @@
         return (zk, zu)
 
     for h in (0, 1):
+        for i in range(3):
+            early_load(h, i).wait()
         zc = _half(X, h, lambda x, pos, zl, zc: prep(x, pos, zl, zc, h), (zero_z(), zero_z()))
         store_z(0, h, zc[0])
         store_z(1, h, zc[1])
@@ -253,6 +273,9 @@
         last = n == ITERS - 1
         src, out = us[n], (la if last else us[n + 1])
         e_in, e_out = 1 + n, 2 + n
+        if last:
+            for i, (src_hbm, dst) in enumerate(late):
+                load(6 + i, src_hbm, dst).wait()
 
         def fwd(x, pos, zl, zc, h):
             c, nb = _slab_nbrs(g, src, halo(e_in, h), x, pos, zl)
@@ -298,13 +321,16 @@
     X, Y, Z = checkpoint.shape
     field = jax.ShapeDtypeStruct((X, Y, Z), jnp.float32)
     f32 = jnp.float32
-    in_specs = [_vmem(), _vmem(), _smem(), _vmem(), _vmem(), _vmem(), _vmem()]
+    hbm = pl.BlockSpec(memory_space=pl.ANY)
+    in_specs = [hbm, hbm, _smem(), hbm, hbm, hbm, hbm]
+    i32 = jnp.int32
     return pl.pallas_call(
         functools.partial(_window_kernel, sizes),
         out_shape=(field, field),
         in_specs=in_specs,
         out_specs=(_vmem(), _vmem()),
-        scratch_shapes=[pltpu.VMEM((X, Y, Z), f32), pltpu.VMEM((6, X, Y, Z), f32)]
+        scratch_shapes=[pltpu.VMEM((X, Y, Z), t) for t in (f32, f32, i32, f32, i32, f32)]
+        + [pltpu.VMEM((X, Y, Z), f32), pltpu.VMEM((6, X, Y, Z), f32)]
         + [pltpu.VMEM((X, Y, Z), f32) for _ in range(5)]
         + [
             pltpu.VMEM((N_EX, 2, Y, Z), f32),
@@ -315,6 +341,7 @@
             pltpu.VMEM((N_EX, 2, 2, Y, LANES), f32),
             pltpu.SemaphoreType.DMA((N_EX, N_COPY)),
             pltpu.SemaphoreType.DMA((N_EX, N_COPY)),
+            pltpu.SemaphoreType.DMA((9,)),
         ],
         compiler_params=pltpu.CompilerParams(
             vmem_limit_bytes=VMEM_LIMIT, collective_id=0, has_side_effects=True

time: 86.9 us -> 83.1 us (0.956)
  Pallas kernels: 81.6 us -> 77.7 us
    pallas_call x1, Pallas kernels: 81.6 us -> 77.7 us  [_shards(): pl.pallas_call(functools.partial(_window_kernel, sizes), out_shape=(field...]
where the time goes in v6:
time: 83.1 us; the launch traced here: 83 us
  Pallas kernels  77.7 us (94%)
  local copies, waits for them, and re-layouts  4.6 us (6%)
    pallas_call x1, Pallas kernels, _shards(): pl.pallas_call(functools.partial(_window_kernel, sizes), out_shape=(field...  77.7 us
    unnamed x4, local copies, waits for them, and re-layouts  4.6 us

profile of v6, /device:TPU:99, one launch (start us, length us, event | category | flops | bytes accessed | tf_op | source)
XLA Modules:
  0.0 83.0 jit_solution(17616351559211857526)
XLA Ops:
  0.6 77.7 %shard_map.86 = (f32[32,64,256]{2,1,0:T(8,128)}, f32[32,64,256]{2,1,0:T(8,128)}) custom-call(f32[32,64,256]{2,1,0:T(8,128)} %ckpt_hbm.1, f32[32,64,256]{2,1,0:T(8,128)} %diff_hbm.1, f32[4]{0:T(128)} %scale.1, s32[32,64,256]{2,1,0:T(8,128)} %labels_hbm.1, f32[32,64,256]{2,1,0:T(8,128)} %meas_hbm.1, s32[32,64,256]{2,1,0:T(8,128)} %obs_hbm.1, ...), custom_call_target="tpu_custom_call" | custom-call | tf_op jit(solution)/shard_map/pallas_call | solution.py:327
  78.4 0.0 copy-start
  78.4 3.3 %copy.11 = f32[32,64,256]{2,1,0:T(8,128)} copy(f32[32,64,256]{2,1,0:T(8,128)} %get-tuple-element.4) | data formatting | bytes 4194304
  81.7 0.0 copy-done
  81.7 1.3 %copy.12 = f32[32,64,256]{2,1,0:T(8,128)} copy(f32[32,64,256]{2,1,0:T(8,128)S(1)} %copy-done) | data formatting | bytes 4194304
Async XLA Ops:
  78.4 3.3 %copy-start = (f32[32,64,256]{2,1,0:T(8,128)S(1)}, f32[32,64,256]{2,1,0:T(8,128)}, u32[]{:S(2)}) copy-start(f32[32,64,256]{2,1,0:T(8,128)} %get-tuple-element.5) | copy-start | bytes 6291460

commit v7 on v6

--- a/solution.py
+++ b/solution.py
@@ -45,9 +45,9 @@
     xm = xh[0] if pos == "first" else F[x - 1]
     xp = xh[1] if pos == "last" else F[x + 1]
     ym = pltpu.roll(c, 1, 0)
-    ym = jnp.concatenate([jnp.where(g.row8 == 0, yh[0, pl.ds(x, 1), :], ym[0:8]), ym[8:]], axis=0)
+    ym = jnp.concatenate([jnp.where(g.row8 == 0, yh[0, pl.ds(zl, 1), :], ym[0:8]), ym[8:]], axis=0)
     yp = pltpu.roll(c, Y - 1, 0)
-    yp = jnp.concatenate([yp[: Y - 8], jnp.where(g.row8 == 7, yh[1, pl.ds(x, 1), :], yp[Y - 8 :])], axis=0)
+    yp = jnp.concatenate([yp[: Y - 8], jnp.where(g.row8 == 7, yh[1, pl.ds(zl, 1), :], yp[Y - 8 :])], axis=0)
     zlo = pltpu.roll(zh[0], lax.rem(LANES - zl, LANES), 1)
     zhi = pltpu.roll(zh[1], lax.rem(LANES - 1 - zl + LANES, LANES), 1)
     zm = pltpu.roll(c, 1, 1)
@@ -65,23 +65,27 @@
         xs[0] = new
     if pos == "last":
         xs[1] = new
-    ys[0, pl.ds(x, 1), :] = new[0:1, :]
-    ys[1, pl.ds(x, 1), :] = new[g.Y - 1 : g.Y, :]
+    ys[0, pl.ds(zl, 1), :] = new[0:1, :]
+    ys[1, pl.ds(zl, 1), :] = new[g.Y - 1 : g.Y, :]
     w0 = pltpu.roll(new[:, 0:LANES], zl, 1)
     w1 = pltpu.roll(new[:, g.Z - LANES : g.Z], lax.rem(zl + 1, LANES), 1)
     z0, z1 = zc
     return (jnp.where(g.lane128 == zl, w0, z0), jnp.where(g.lane128 == zl, w1, z1))
 
 
-def _half(X, h, body, carry):
+def _groups(X):
     H = X // 2
-    if h == 0:
-        if H > 1:
-            carry = lax.fori_loop(1, H, lambda x, c: body(x, "mid", x, c), carry)
-        return body(0, "first", 0, carry)
-    if X - 1 > H:
-        carry = lax.fori_loop(H, X - 1, lambda x, c: body(x, "mid", x - H, c), carry)
-    return body(X - 1, "last", X - 1 - H, carry)
+    return ((None, 2), (1, H - 1), (H, X - 1 - H))
+
+
+def _group(X, gi, body, carry):
+    if gi == 0:
+        carry = body(0, "first", 0, carry)
+        return body(X - 1, "last", 1, carry)
+    x0, n = _groups(X)[gi]
+    if n > 0:
+        carry = lax.fori_loop(x0, x0 + n, lambda x, c: body(x, "mid", x - x0, c), carry)
+    return carry
 
 
 def _factor(scale, lab):
@@ -98,7 +102,7 @@
 
 
 N_EX = 2 * ITERS + 1
-N_COPY = 10
+N_COPY = 14
 
 
 def _window_kernel(
@@ -110,8 +114,8 @@
 ):
     g = Geo(ckpt.shape)
     X = g.X
-    H = X // 2
-    halves = (pl.ds(0, H), pl.ds(H, X - H))
+    chunks = (pl.ds(0, 1), pl.ds(X - 1, 1)) + tuple(pl.ds(x0, n) for x0, n in _groups(X)[1:] if n > 0)
+    n_chunk = len(chunks)
     early = ((ckpt_hbm, ckpt), (diff_hbm, diff), (labels_hbm, labels))
     late = ((meas_hbm, meas), (obs_hbm, obs), (adj_hbm, adj))
 
@@ -120,15 +124,21 @@
             src, dst = src.at[rows], dst.at[rows]
         return pltpu.make_async_copy(src, dst, load_sem.at[i])
 
-    def early_load(h, i):
+    def early_load(c, i):
         src, dst = early[i]
-        return load(2 * i + h, src, dst, halves[h])
-
-    for h in (0, 1):
+        return load(n_chunk * i + c, src, dst, chunks[c])
+
+    def group_chunks(gi):
+        if gi == 0:
+            return (0, 1)
+        return tuple(c for c in range(2, n_chunk) if c - 1 == gi)
+
+    for c in range(n_chunk):
         for i in range(3):
-            early_load(h, i).start()
+            early_load(c, i).start()
     for i, (src, dst) in enumerate(late):
-        load(6 + i, src, dst).start()
+        load(3 * n_chunk + i, src, dst).start()
+
     idx = [lax.axis_index(a) for a in AXES]
 
     def nbr(a, d):
@@ -139,18 +149,17 @@
     def has(a, d):
         return jnp.logical_and(idx[a] + d >= 0, idx[a] + d < sizes[a])
 
-    for a, dst in enumerate((xh, yh)):
-        for s, d in ((0, -1), (1, 1)):
+    for s, d in ((0, -1), (1, 1)):
+
+        @pl.when(jnp.logical_not(has(0, d)))
+        def _():
+            xh[:, s] = jnp.zeros(xh.shape[:1] + xh.shape[2:], xh.dtype)
+
+        for a, dst in ((1, yh), (2, zh)):
 
             @pl.when(jnp.logical_not(has(a, d)))
             def _():
-                dst[:, s] = jnp.zeros(dst.shape[:1] + dst.shape[2:], dst.dtype)
-
-    for s, d in ((0, -1), (1, 1)):
-
-        @pl.when(jnp.logical_not(has(2, d)))
-        def _():
-            zh[:, :, s] = jnp.zeros(zh.shape[:2] + zh.shape[3:], zh.dtype)
+                dst[:, :, s] = jnp.zeros(dst.shape[:2] + dst.shape[3:], dst.dtype)
 
     barrier = pltpu.get_barrier_semaphore()
     count = jnp.int32(0)
@@ -167,13 +176,12 @@
     def copy(e, k):
         if k < 2:
             a, s, src, dst = 0, k, xs.at[e, 1 - k], xh.at[e, k]
-        elif k < 6:
-            h, s = divmod(k - 2, 2)
-            rows = pl.ds(h * H, H) if h == 0 else pl.ds(H, X - H)
-            a, src, dst = 1, ys.at[e, 1 - s, rows], yh.at[e, s, rows]
         else:
-            h, s = divmod(k - 6, 2)
-            a, src, dst = 2, zs.at[e, h, 1 - s], zh.at[e, h, s]
+            gi, r = divmod(k - 2, 4)
+            kind, s = divmod(r, 2)
+            a = 1 + kind
+            buf_s, buf_h = (ys, yh) if kind == 0 else (zs, zh)
+            src, dst = buf_s.at[e, gi, 1 - s], buf_h.at[e, gi, s]
         d = 1 if s == 0 else -1
         desc = pltpu.make_async_remote_copy(
             src_ref=src,
@@ -209,56 +217,51 @@
             def _():
                 desc.wait_send()
 
-    SENT = ((1, 2, 3, 6, 7), (0, 4, 5, 8, 9))
-    NEED = ((2, 3, 6, 7), (1, 4, 5, 8, 9))
-
-    def faces(e):
-        return (xs.at[e], ys.at[e])
-
-    def halo(e, h):
-        return (xh.at[e], yh.at[e], zh.at[e, h])
+    def group_copies(gi):
+        return tuple(2 + 4 * gi + r for r in range(4)) + ((0, 1) if gi == 0 else ())
+
+    def faces(e, gi):
+        return (xs.at[e], ys.at[e, gi])
+
+    def halo(e, gi):
+        return (xh.at[e], yh.at[e, gi], zh.at[e, gi])
 
     def zero_z():
         z = jnp.zeros((g.Y, LANES), jnp.float32)
         return (z, z)
 
-    def store_z(e, h, zc):
-        zs[e, h, 0] = zc[0]
-        zs[e, h, 1] = zc[1]
+    def store_z(e, gi, zc):
+        zs[e, gi, 0] = zc[0]
+        zs[e, gi, 1] = zc[1]
 
     def sweep(e_in, e_out, body):
-        for h in (0, 1):
+        for gi in range(3):
             if e_in is not None:
-                wait_recv(e_in, NEED[h])
-                if h == 1:
-                    wait_send(e_in, range(N_COPY))
-
-            def run(x, pos, zl, zc):
-                if pos == "first" and e_in is not None:
-                    wait_recv(e_in, (0,))
-                return body(x, pos, zl, zc, h)
-
-            zc = _half(X, h, run, zero_z())
+                wait_recv(e_in, group_copies(gi))
+            zc = _group(X, gi, lambda x, pos, zl, zc: body(x, pos, zl, zc, gi), zero_z())
             if e_out is not None:
-                store_z(e_out, h, zc)
-                start(e_out, SENT[h])
-
-    def prep(x, pos, zl, zc, h):
+                store_z(e_out, gi, zc)
+                start(e_out, group_copies(gi))
+        if e_in is not None:
+            wait_send(e_in, range(N_COPY))
+
+    def prep(x, pos, zl, zc, gi):
         k = diff[x] * _factor(scale, labels[x])
         kap[x] = k
         zk, zu = zc
-        zk = _pack(g, faces(0), x, k, pos, zl, zk)
-        zu = _pack(g, faces(1), x, ckpt[x], pos, zl, zu)
+        zk = _pack(g, faces(0, gi), x, k, pos, zl, zk)
+        zu = _pack(g, faces(1, gi), x, ckpt[x], pos, zl, zu)
         return (zk, zu)
 
-    for h in (0, 1):
-        for i in range(3):
-            early_load(h, i).wait()
-        zc = _half(X, h, lambda x, pos, zl, zc: prep(x, pos, zl, zc, h), (zero_z(), zero_z()))
-        store_z(0, h, zc[0])
-        store_z(1, h, zc[1])
-        start(0, SENT[h])
-        start(1, SENT[h])
+    for gi in range(3):
+        for c in group_chunks(gi):
+            for i in range(3):
+                early_load(c, i).wait()
+        zc = _group(X, gi, lambda x, pos, zl, zc: prep(x, pos, zl, zc, gi), (zero_z(), zero_z()))
+        store_z(0, gi, zc[0])
+        store_z(1, gi, zc[1])
+        start(0, group_copies(gi))
+        start(1, group_copies(gi))
 
     def conduct(x, pos, zl, zc, h):
         kc, knb = _slab_nbrs(g, kap, halo(0, h), x, pos, zl)
@@ -275,7 +278,7 @@
         e_in, e_out = 1 + n, 2 + n
         if last:
             for i, (src_hbm, dst) in enumerate(late):
-                load(6 + i, src_hbm, dst).wait()
+                load(3 * n_chunk + i, src_hbm, dst).wait()
 
         def fwd(x, pos, zl, zc, h):
             c, nb = _slab_nbrs(g, src, halo(e_in, h), x, pos, zl)
@@ -283,7 +286,7 @@
             if last:
                 new = adj[x] + obs[x].astype(jnp.float32) * (new - meas[x])
             out[x] = new
-            return _pack(g, faces(e_out), x, new, pos, zl, zc)
+            return _pack(g, faces(e_out, h), x, new, pos, zl, zc)
 
         sweep(e_in, e_out, fwd)
 
@@ -312,7 +315,7 @@
             out[x] = new
             if final:
                 return zc
-            return _pack(g, faces(e_out), x, new, pos, zl, zc)
+            return _pack(g, faces(e_out, h), x, new, pos, zl, zc)
 
         sweep(e_lam, None if final else e_out, bwd)
 
@@ -321,6 +324,7 @@
     X, Y, Z = checkpoint.shape
     field = jax.ShapeDtypeStruct((X, Y, Z), jnp.float32)
     f32 = jnp.float32
+    rows = -(-max(n for _, n in _groups(X)) // 8) * 8
     hbm = pl.BlockSpec(memory_space=pl.ANY)
     in_specs = [hbm, hbm, _smem(), hbm, hbm, hbm, hbm]
     i32 = jnp.int32
@@ -334,14 +338,14 @@
         + [pltpu.VMEM((X, Y, Z), f32) for _ in range(5)]
         + [
             pltpu.VMEM((N_EX, 2, Y, Z), f32),
-            pltpu.VMEM((N_EX, 2, X, Z), f32),
-            pltpu.VMEM((N_EX, 2, 2, Y, LANES), f32),
+            pltpu.VMEM((N_EX, 3, 2, rows, Z), f32),
+            pltpu.VMEM((N_EX, 3, 2, Y, LANES), f32),
             pltpu.VMEM((N_EX, 2, Y, Z), f32),
-            pltpu.VMEM((N_EX, 2, X, Z), f32),
-            pltpu.VMEM((N_EX, 2, 2, Y, LANES), f32),
+            pltpu.VMEM((N_EX, 3, 2, rows, Z), f32),
+            pltpu.VMEM((N_EX, 3, 2, Y, LANES), f32),
             pltpu.SemaphoreType.DMA((N_EX, N_COPY)),
             pltpu.SemaphoreType.DMA((N_EX, N_COPY)),
-            pltpu.SemaphoreType.DMA((9,)),
+            pltpu.SemaphoreType.DMA((3 * 4 + 3,)),
         ],
         compiler_params=pltpu.CompilerParams(
             vmem_limit_bytes=VMEM_LIMIT, collective_id=0, has_side_effects=True

time: 83.1 us -> 80.1 us (0.964)
  the two profiles are of different devices: /device:TPU:99 before, /device:TPU:0 now
where the time goes in v7:
time: 80.1 us; the launch traced here: 78.6 us
  Pallas kernels  73.3 us (92%)
  local copies, waits for them, and re-layouts  4.6 us (6%)
    pallas_call x1, Pallas kernels, _shards(): pl.pallas_call(functools.partial(_window_kernel, sizes), out_shape=(field...  73.3 us
    unnamed x4, local copies, waits for them, and re-layouts  4.6 us

profile of v7, /device:TPU:0, one launch (start us, length us, event | category | flops | bytes accessed | tf_op | source)
XLA Modules:
  0.0 78.6 jit_solution(9518068563357649837)
XLA Ops:
  0.6 73.3 %shard_map.86 = (f32[32,64,256]{2,1,0:T(8,128)}, f32[32,64,256]{2,1,0:T(8,128)}) custom-call(f32[32,64,256]{2,1,0:T(8,128)} %ckpt_hbm.1, f32[32,64,256]{2,1,0:T(8,128)} %diff_hbm.1, f32[4]{0:T(128)} %scale.1, s32[32,64,256]{2,1,0:T(8,128)} %labels_hbm.1, f32[32,64,256]{2,1,0:T(8,128)} %meas_hbm.1, s32[32,64,256]{2,1,0:T(8,128)} %obs_hbm.1, ...), custom_call_target="tpu_custom_call" | custom-call | tf_op jit(solution)/shard_map/pallas_call | solution.py:331
  74.0 0.0 copy-start
  74.0 3.3 %copy.11 = f32[32,64,256]{2,1,0:T(8,128)} copy(f32[32,64,256]{2,1,0:T(8,128)} %get-tuple-element.4) | data formatting | bytes 4194304
  77.3 0.0 copy-done
  77.3 1.3 %copy.12 = f32[32,64,256]{2,1,0:T(8,128)} copy(f32[32,64,256]{2,1,0:T(8,128)S(1)} %copy-done) | data formatting | bytes 4194304
Async XLA Ops:
  74.0 3.3 %copy-start = (f32[32,64,256]{2,1,0:T(8,128)S(1)}, f32[32,64,256]{2,1,0:T(8,128)}, u32[]{:S(2)}) copy-start(f32[32,64,256]{2,1,0:T(8,128)} %get-tuple-element.5) | copy-start | bytes 6291460

commit v8 on v7

--- a/solution.py
+++ b/solution.py
@@ -218,7 +218,7 @@
                 desc.wait_send()
 
     def group_copies(gi):
-        return tuple(2 + 4 * gi + r for r in range(4)) + ((0, 1) if gi == 0 else ())
+        return ((0, 1) if gi == 0 else ()) + tuple(2 + 4 * gi + r for r in range(4))
 
     def faces(e, gi):
         return (xs.at[e], ys.at[e, gi])

time: 80.1 us -> 79.7 us (level)
  no operation moved by 1% of the time
where the time goes in v8:
time: 79.7 us; the launch traced here: 78.3 us
  Pallas kernels  73.1 us (92%)
  local copies, waits for them, and re-layouts  4.6 us (6%)
    pallas_call x1, Pallas kernels, _shards(): pl.pallas_call(functools.partial(_window_kernel, sizes), out_shape=(field...  73.1 us
    unnamed x4, local copies, waits for them, and re-layouts  4.6 us

profile of v8, /device:TPU:0, one launch (start us, length us, event | category | flops | bytes accessed | tf_op | source)
XLA Modules:
  0.0 78.3 jit_solution(1797055350739145281)
XLA Ops:
  0.6 73.1 %shard_map.86 = (f32[32,64,256]{2,1,0:T(8,128)}, f32[32,64,256]{2,1,0:T(8,128)}) custom-call(f32[32,64,256]{2,1,0:T(8,128)} %ckpt_hbm.1, f32[32,64,256]{2,1,0:T(8,128)} %diff_hbm.1, f32[4]{0:T(128)} %scale.1, s32[32,64,256]{2,1,0:T(8,128)} %labels_hbm.1, f32[32,64,256]{2,1,0:T(8,128)} %meas_hbm.1, s32[32,64,256]{2,1,0:T(8,128)} %obs_hbm.1, ...), custom_call_target="tpu_custom_call" | custom-call | tf_op jit(solution)/shard_map/pallas_call | solution.py:331
  73.7 0.0 copy-start
  73.7 3.3 %copy.11 = f32[32,64,256]{2,1,0:T(8,128)} copy(f32[32,64,256]{2,1,0:T(8,128)} %get-tuple-element.4) | data formatting | bytes 4194304
  77.0 0.0 copy-done
  77.0 1.3 %copy.12 = f32[32,64,256]{2,1,0:T(8,128)} copy(f32[32,64,256]{2,1,0:T(8,128)S(1)} %copy-done) | data formatting | bytes 4194304
Async XLA Ops:
  73.7 3.3 %copy-start = (f32[32,64,256]{2,1,0:T(8,128)S(1)}, f32[32,64,256]{2,1,0:T(8,128)}, u32[]{:S(2)}) copy-start(f32[32,64,256]{2,1,0:T(8,128)} %get-tuple-element.5) | copy-start | bytes 6291460
